TPU v7x, 128 devices: a whole 4x4x4 slice. The times are simulated.
128 devices in a mesh: ty: 8 (over x, core), tx: 16 (over y, z).
Axes of the slice: x: 4, y: 4, z: 4, core: 2. Of those that a mesh axis runs over, the one named last changes fastest.
Arguments:
- roi_feat: bfloat16 [1536, 14, 14, 256], P(('ty', 'tx')), may hold values from -6 to 6
- pre_one: bfloat16 [1536, 14, 14, 256], P(('ty', 'tx')), may hold values from -6 to 6
- grad_two: bfloat16 [1536, 14, 14, 256], P(('ty', 'tx')), may hold values from -24 to 24
- w_one: bfloat16 [3, 3, 256, 256], replicated, may hold values from -0.125 to 0.125
- w_two: bfloat16 [3, 3, 256, 256], replicated, may hold values from -0.125 to 0.125
- roi_rows: bfloat16 [1536, 16, 14], P(('ty', 'tx')), may hold values from -1.5 to 1.5
- roi_cols: bfloat16 [1536, 16, 14], P(('ty', 'tx')), may hold values from -1.5 to 1.5
- target_col: int32 [1536, 1], P(('ty', 'tx')), may hold values from 0 to 15; in each aligned block of 12 rows (0 to 11, 12 to 23, ...) at most 2 rows name the same one
- off_row: int32 [1536], P(('ty', 'tx')), may hold values from 0 to 15
- off_col: int32 [1536], P(('ty', 'tx')), may hold values from 0 to 63
- fpn_input: bfloat16 [128, 1024, 256], P('ty', 'tx'), may hold values from -6 to 6
- fpn_grad: bfloat16 [128, 1024, 256], P('ty', 'tx'), may hold values from -6 to 6
- w_fpn: bfloat16 [3, 3, 256, 256], replicated, may hold values from -0.125 to 0.125
Outputs:
- grad_fpn_input: bfloat16 [128, 1024, 256], P('ty', 'tx')
- grad_w_one: float32 [589824], P(('ty', 'tx'))
- grad_w_two: float32 [589824], P(('ty', 'tx'))
- grad_w_fpn: float32 [589824], P(('ty', 'tx'))
Inputs may be any that keep to these rules, and one draw needn't show every extreme that they name: `target_col`: at most 2 regions of one device name the same column, and in every draw some device names some column exactly 2 times.
All inputs are finite; a program needn't handle non-finite values.
Results may differ from a plain program's by a relative error of at most 0.0075.
Values may be sent and summed in bfloat16 or wider, within the bound.
A program may use at most 128 MiB of HBM per device.

v0:
```python
import jax
import jax.numpy as jnp
from jax import lax
from jax.sharding import PartitionSpec as P


def shifted(shard, axis, by):
    devices = lax.axis_size(axis)
    pairs = [(i, i + by) for i in range(devices) if 0 <= i + by < devices]
    return lax.ppermute(shard, axis, pairs)


def extended(block, sides, width):
    for axis, dim in sides:
        count = lax.axis_size(axis)
        forward = [(i, i + 1) for i in range(count - 1)]
        backward = [(target, source) for source, target in forward]
        low = lax.ppermute(
            lax.slice_in_dim(block, block.shape[dim] - width, None, axis=dim), axis, forward
        )
        high = lax.ppermute(lax.slice_in_dim(block, 0, width, axis=dim), axis, backward)
        block = jnp.concatenate([low, block, high], axis=dim)
    return block


def window_patches(padded, row_count, col_count, flipped):
    pieces = []
    for row_step in range(3):
        for col_step in range(3):
            row_start = 2 - row_step if flipped else row_step
            col_start = 2 - col_step if flipped else col_step
            pieces.append(
                padded[..., row_start : row_start + row_count, col_start : col_start + col_count, :]
            )
    return jnp.concatenate(pieces, axis=-1)


def flipped_weight(weight):
    channels = weight.shape[2]
    return jnp.transpose(weight, (0, 1, 3, 2)).reshape(9 * channels, channels)


def weight_term(gradient, inputs_patch):
    return lax.dot_general(
        gradient, inputs_patch, (((0,), (0,)), ((), ())), preferred_element_type=jnp.float32
    )


def region_windows(region_grad, row_weights, col_weights):
    highest = lax.Precision.HIGHEST
    partial_sum = jnp.einsum(
        "nxj,nijc->nixc",
        col_weights.astype(jnp.float32),
        region_grad.astype(jnp.float32),
        precision=highest,
    )
    return jnp.einsum(
        "nyi,nixc->nyxc", row_weights.astype(jnp.float32), partial_sum, precision=highest
    ).astype(jnp.bfloat16)


def place_windows(windows, offsets, row_count, col_count):
    extent = windows.shape[1]
    inside = jnp.arange(extent, dtype=jnp.int32)[None, None, :]
    row_hit = (
        jnp.arange(row_count + extent, dtype=jnp.int32)[None, :, None]
        == offsets[:, 0][:, None, None] + inside
    ).astype(jnp.bfloat16)
    col_hit = (
        jnp.arange(col_count + extent, dtype=jnp.int32)[None, :, None]
        == offsets[:, 1][:, None, None] + inside
    ).astype(jnp.bfloat16)
    spread = jnp.einsum(
        "sXx,syxc->syXc", col_hit, windows, preferred_element_type=jnp.float32
    ).astype(jnp.bfloat16)
    return jnp.einsum("sYy,syXc->YXc", row_hit, spread, preferred_element_type=jnp.float32)


def local(
    roi_feat,
    pre_one,
    grad_two,
    w_one,
    w_two,
    roi_rows,
    roi_cols,
    target_col,
    off_row,
    off_col,
    fpn_input,
    fpn_grad,
    w_fpn,
):
    region_count, pool_size, channels = (roi_feat.shape[0], roi_feat.shape[1], roi_feat.shape[3])
    tile_rows, tile_cols = (fpn_input.shape[0], fpn_input.shape[1])
    extent = roi_rows.shape[1]
    columns = lax.axis_size("tx")
    capacity = max(2, (2 * region_count + columns - 1) // columns)
    positions = region_count * pool_size * pool_size
    region_pad = ((0, 0), (1, 1), (1, 1), (0, 0))
    active = jnp.maximum(pre_one, 0)
    back_two = jnp.dot(
        window_patches(jnp.pad(grad_two, region_pad), pool_size, pool_size, True).reshape(
            positions, 9 * channels
        ),
        flipped_weight(w_two),
        preferred_element_type=jnp.float32,
    )
    grad_one = jnp.where(pre_one.reshape(positions, channels) > 0, back_two, 0.0).astype(
        jnp.bfloat16
    )
    term_two = weight_term(
        grad_two.reshape(positions, channels),
        window_patches(jnp.pad(active, region_pad), pool_size, pool_size, False).reshape(
            positions, 9 * channels
        ),
    )
    term_one = weight_term(
        grad_one,
        window_patches(jnp.pad(roi_feat, region_pad), pool_size, pool_size, False).reshape(
            positions, 9 * channels
        ),
    )
    region_grad = (
        jnp.dot(
            window_patches(
                jnp.pad(grad_one.reshape(region_count, pool_size, pool_size, channels), region_pad),
                pool_size,
                pool_size,
                True,
            ).reshape(positions, 9 * channels),
            flipped_weight(w_one),
            preferred_element_type=jnp.float32,
        )
        .astype(jnp.bfloat16)
        .reshape(region_count, pool_size, pool_size, channels)
    )
    targets = target_col[:, 0]
    order_ids = jnp.arange(region_count, dtype=jnp.int32)
    earlier = order_ids[None, :] < order_ids[:, None]
    slot_rank = jnp.sum(
        ((targets[None, :] == targets[:, None]) & earlier).astype(jnp.int32), axis=1
    )
    slot_index = targets * capacity + slot_rank
    selector = (
        jnp.arange(columns * capacity, dtype=jnp.int32)[:, None] == slot_index[None, :]
    ).astype(jnp.bfloat16)
    offsets = jnp.stack([off_row, off_col], axis=1).astype(jnp.bfloat16)

    def pack_slots(values):
        flattened = values.reshape(region_count, -1)
        packed = jnp.dot(selector, flattened, preferred_element_type=jnp.float32).astype(
            jnp.bfloat16
        )
        return packed.reshape((columns, capacity) + values.shape[1:])

    windows = region_windows(region_grad, roi_rows, roi_cols)
    received, got_offsets = (
        lax.all_to_all(pack_slots(windows), "tx", split_axis=0, concat_axis=0, tiled=True),
        lax.all_to_all(pack_slots(offsets), "tx", split_axis=0, concat_axis=0, tiled=True),
    )
    slot_total = columns * capacity
    windows_in = received.reshape((slot_total,) + received.shape[2:])
    place_at = got_offsets.reshape(slot_total, 2).astype(jnp.int32)
    canvas = place_windows(windows_in, place_at, tile_rows, tile_cols)
    spill_right = shifted(canvas[:, tile_cols:, :].astype(jnp.bfloat16), "tx", 1).astype(
        jnp.float32
    )
    canvas = canvas[:, :tile_cols, :].at[:, :extent, :].add(spill_right)
    spill_low = shifted(canvas[tile_rows:, :, :].astype(jnp.bfloat16), "ty", 1).astype(jnp.float32)
    canvas = canvas[:tile_rows].at[:extent].add(spill_low)
    feature_grad = (fpn_grad.astype(jnp.float32) + canvas).astype(jnp.bfloat16)
    grad_padded, input_padded = (
        extended(feature_grad, (("ty", 0), ("tx", 1)), 1),
        extended(fpn_input, (("ty", 0), ("tx", 1)), 1),
    )
    tile_positions = tile_rows * tile_cols
    input_grad = (
        jnp.dot(
            window_patches(grad_padded, tile_rows, tile_cols, True).reshape(
                tile_positions, 9 * channels
            ),
            flipped_weight(w_fpn),
            preferred_element_type=jnp.float32,
        )
        .astype(jnp.bfloat16)
        .reshape(tile_rows, tile_cols, channels)
    )
    term_fpn = weight_term(
        feature_grad.reshape(tile_positions, channels),
        window_patches(input_padded, tile_rows, tile_cols, False).reshape(
            tile_positions, 9 * channels
        ),
    )
    head_one, head_two, fpn_total = (
        lax.psum_scatter(term_one.reshape(-1), ("ty", "tx"), scatter_dimension=0, tiled=True),
        lax.psum_scatter(term_two.reshape(-1), ("ty", "tx"), scatter_dimension=0, tiled=True),
        lax.psum_scatter(term_fpn.reshape(-1), ("ty", "tx"), scatter_dimension=0, tiled=True),
    )
    return (input_grad, head_one, head_two, fpn_total)


def solution(mesh):
    placed = (
        P(("ty", "tx"), None, None, None),
        P(("ty", "tx"), None, None, None),
        P(("ty", "tx"), None, None, None),
        P(),
        P(),
        P(("ty", "tx"), None, None),
        P(("ty", "tx"), None, None),
        P(("ty", "tx"), None),
        P(("ty", "tx")),
        P(("ty", "tx")),
        P("ty", "tx", None),
        P("ty", "tx", None),
        P(),
    )
    return jax.shard_map(
        local,
        mesh=mesh,
        in_specs=placed,
        out_specs=(P("ty", "tx", None), P(("ty", "tx")), P(("ty", "tx")), P(("ty", "tx"))),
        check_vma=False,
    )
```

profile of v0, /device:TPU:0, one launch (start us, length us, event | category | flops | bytes accessed | tf_op | source)
XLA Modules:
  0.0 467.9 jit_solution(7768226116081704984)
XLA Ops:
  10.3 8.2 %all-to-all-start = ((bf16[16,2,2]{1,2,0:T(2,128)(2,1)}), bf16[16,2,2]{1,2,0:T(2,128)(2,1)S(1)}, u32[]{:S(2)}, u32[]{:S(2)}) async-start(bf16[16,2,2]{1,2,0:T(2,128)(2,1)} %copy.62), calls=%async_computation | async-start | bytes 16384 | tf_op jit(solution)/shard_map/all_to_all | solution.py:160
  18.5 1.4 copy.73
  20.6 1.4 collective-permute-start.6
  22.1 1.4 collective-permute-start.7
  23.5 2.5 broadcast_compare_fusion
  26.2 1.6 slice_dynamic-update-slice_fusion.23
  29.1 1.8 slice_dynamic-update-slice_fusion.21
  30.9 1.7 slice_dynamic-update-slice_fusion.20
  33.8 1.7 slice_dynamic-update-slice_fusion.19
  35.5 1.7 slice_dynamic-update-slice_fusion.18
  38.5 1.8 slice_dynamic-update-slice_fusion.16
  40.2 16.8 %reshape.197 = bf16[2352,2304]{1,0:T(8,128)(2,1)} reshape(bf16[12,14,14,2304]{3,2,1,0:T(8,128)(2,1)} %slice_dynamic-update-slice_fusion.16) | data formatting | bytes 21676032 | tf_op jit(solution)/shard_map/reshape | solution.py:103
  57.1 2.8 gt.11
  59.9 2.4 copy.65
  62.3 8.5 %fusion.2 = bf16[2352,256]{1,0:T(8,128)(2,1)} fusion(pred[2352,256]{1,0:T(8,128)(4,1)} %gt.11, bf16[2352,2304]{1,0:T(8,128)(2,1)} %reshape.197, bf16[2304,256]{1,0:T(8,128)(2,1)} %bitcast.91), kind=kOutput, calls=%fused_computation.8 | convolution fusion | flops 2775736320 | bytes 13824000 | tf_op jit(solution)/shard_map/dot_general | solution.py:102
  70.9 3.1 reshape.199
  73.9 8.7 %pad_slice_fusion = (bf16[12,14,14,256]{3,2,1,0:T(8,128)(2,1)}, bf16[12,14,14,256]{3,2,1,0:T(8,128)(2,1)}, bf16[12,14,14,256]{3,2,1,0:T(8,128)(2,1)}, bf16[12,14...) fusion(bf16[12,14,14,256]{3,2,1,0:T(8,128)(2,1)} %reshape.199), kind=kLoop, calls=%fused_computation.45 | loop fusion | bytes 10838016 | tf_op jit(solution)/shard_map/slice | solution.py:33
  82.6 3.0 concatenate.80
  85.7 2.5 constant_dynamic-update-slice_fusion.9
  88.2 3.0 concatenate.81
  91.2 3.0 concatenate.82
  94.2 3.0 concatenate.83
  97.3 2.7 constant_dynamic-update-slice_fusion.8
  103.5 3.0 concatenate.84
  106.5 3.0 concatenate.85
  109.6 3.0 concatenate.86
  112.6 3.0 concatenate.87
  115.6 2.4 copy.66
  118.0 2.6 constant_dynamic-update-slice_fusion.4
  124.3 8.1 %convolution_convert_fusion.1 = bf16[2352,256]{1,0:T(8,128)(2,1)} fusion(bf16[2352,2304]{1,0:T(8,128)(2,1)} %constant_dynamic-update-slice_fusion.1, bf16[2304,256]{1,0:T(8,128)(2,1)S(1)} %bitcast.90), kind=kOutput, calls=%fused_computation.6 | convolution fusion | flops 2775134208 | bytes 13221888 | tf_op jit(solution)/shard_map/dot_general | solution.py:125
  132.4 3.4 reshape.201
  135.8 1.8 convolution_bitcast_fusion.2
  137.7 3.6 fusion.11
  148.2 5.5 %convolution_bitcast_fusion.1 = f32[256,2304]{0,1:T(8,128)} fusion(bf16[12,14,14,2304]{3,2,1,0:T(8,128)(2,1)S(1)} %slice_dynamic-update-slice_fusion, bf16[12,14,14,256]{3,2,1,0:T(8,128)(2,1)S(1)} %copy-done.2), kind=kOutput, calls=%fused_computation.5 | convolution fusion | flops 2774532096 | bytes 14401536 | tf_op jit(solution)/shard_map/dot_general | solution.py:44
  153.7 2.9 copy.85
  156.6 7.2 %all-to-all-start.1 = ((bf16[16,2,16,16,256]{4,3,2,1,0:T(8,128)(2,1)}), bf16[16,2,16,16,256]{4,3,2,1,0:T(8,128)(2,1)}, u32[]{:S(2)}, u32[]{:S(2)}) async-start(bf16[16,2,16,16,256]{4,3,2,1,0:T(8,128)(2,1)} %bitcast.83), calls=%async_computation.1 | async-start | bytes 8388608 | tf_op jit(solution)/shard_map/all_to_all | solution.py:159
  163.9 1.6 slice_dynamic-update-slice_fusion.15
  165.5 3.0 copy.72
  168.6 3.1 reshape.210
  173.0 1.6 slice_dynamic-update-slice_fusion.13
  174.7 1.7 slice_dynamic-update-slice_fusion.12
  177.7 1.6 slice_dynamic-update-slice_fusion.11
  179.3 1.8 slice_dynamic-update-slice_fusion.10
  182.4 1.6 slice_dynamic-update-slice_fusion.8
  184.0 16.7 %reshape.208 = bf16[2352,2304]{1,0:T(8,128)(2,1)} reshape(bf16[12,14,14,2304]{3,2,1,0:T(8,128)(2,1)} %slice_dynamic-update-slice_fusion.8) | data formatting | bytes 21676032 | tf_op jit(solution)/shard_map/reshape | solution.py:120
  200.7 8.8 %fusion.36 = f32[256,2304]{1,0:T(8,128)} fusion(bf16[2352,256]{1,0:T(8,128)(2,1)S(1)} %copy-done.5, bf16[2352,2304]{1,0:T(8,128)(2,1)} %reshape.208), kind=kOutput, calls=%fused_computation.128 | convolution fusion | flops 2774532096 | bytes 14401536 | tf_op jit(solution)/shard_map/dot_general | solution.py:44
  209.5 3.1 reshape.209
  213.0 3.8 collective-permute-start.8
  218.2 4.2 collective-permute-done.9
  227.0 11.8 %convert_bitcast_fusion = bf16[32,16,80,256]{3,2,1,0:T(8,128)(2,1)} fusion(bf16[32,16,16,256]{3,2,1,0:T(8,128)(2,1)} %bitcast.15, s32[32,16]{1,0:T(8,128)S(1)} %iota_add_fusion), kind=kOutput, calls=%fused_computation.3 | convolution fusion | flops 346071040 | bytes 25167872 | tf_op jit(solution)/shard_map/sXx,syxc->syXc/dot_general | solution.py:73
  238.8 20.9 %fusion.5 = f32[32,80,256]{2,0,1:T(8,128)S(1)} fusion(bf16[32,16,80,256]{3,2,1,0:T(8,128)(2,1)} %convert_bitcast_fusion, s32[32,16]{0,1:T(8,128)S(1)} %iota_add_fusion.1), kind=kOutput, calls=%fused_computation.12 | convolution fusion | flops 671105024 | bytes 23595008 | tf_op jit(solution)/shard_map/sYy,syXc->YXc/dot_general | solution.py:76
  259.8 3.6 collective-permute-start
  265.9 3.8 collective-permute-done
  269.9 2.1 collective-permute-start.1
  275.8 3.7 convolution_bitcast_fusion
  279.6 1.6 reshape.211
  281.3 6.6 %collective-permute-start.2 = (bf16[1,64,256]{2,0,1:T(2,128)(2,1)S(1)}, bf16[1,64,256]{2,0,1:T(2,128)(2,1)S(1)}, u32[]{:S(2)}, u32[]{:S(2)}) collective-permute-start(bf16[1,64,256]{2,0,1:T(2,128)(2,1)S(1)} %get-tuple-element.57), channel_id=1, source_target_pairs={{0,16},{16,32},{32,48},{48,64},{64,80},{80,96},{96,112},{1,17},{17... | collective-permute-start | bytes 98312 | tf_op jit(solution)/shard_map/ppermute | solution.py:18
  289.3 3.8 collective-permute-done.3
  294.4 5.0 %collective-permute-start.5 = (bf16[18,1,256]{2,0,1:T(8,128)(2,1)S(1)}, bf16[18,1,256]{2,0,1:T(8,128)(2,1)S(1)}, u32[]{:S(2)}, u32[]{:S(2)}) collective-permute-start(bf16[18,1,256]{2,0,1:T(8,128)(2,1)S(1)} %get-tuple-element.53), channel_id=1, source_target_pairs={{0,1},{1,2},{2,3},{3,4},{4,5},{5,6},{6,7},{7,8},{8,9},{9,10},{10,1... | collective-permute-start | bytes 27656 | tf_op jit(solution)/shard_map/ppermute | solution.py:18
  304.4 2.2 convolution_convert_fusion.2
  306.6 149.8 %all-reduce.10.cloned.1.call-done = (f32[589824]{0:T(1024)}, f32[589824]{0:T(1024)}, f32[589824]{0:T(1024)}) async-done(((f32[589824]{0:T(1024)}, f32[589824]{0:T(1024)}, f32[589824]{0:T(1024)}), (f32[589824]{0:T(1024)}, f32[589824]{0:T(1024)}, f32[589824]{0:T(1024)})) %all-reduce.10.cloned.1.call-update) | async-done | bytes 7077904
  456.4 1.4 dynamic-slice.13
  457.8 1.4 dynamic-slice.14
  459.2 1.4 dynamic-slice.15
  (118 shorter events, 46.4 us)
Async XLA Ops:
  7.2 130.5 %copy-start = (bf16[12,16,14]{2,1,0:T(8,128)(2,1)S(1)}, bf16[12,16,14]{2,1,0:T(8,128)(2,1)}, u32[]{:S(2)}) copy-start(bf16[12,16,14]{2,1,0:T(8,128)(2,1)} %param.24) | copy-start | bytes 16132
  10.3 146.3 %all-to-all-start = ((bf16[16,2,2]{1,2,0:T(2,128)(2,1)}), bf16[16,2,2]{1,2,0:T(2,128)(2,1)S(1)}, u32[]{:S(2)}, u32[]{:S(2)}) async-start(bf16[16,2,2]{1,2,0:T(2,128)(2,1)} %copy.62), calls=%async_computation | async-start | bytes 16384 | tf_op jit(solution)/shard_map/all_to_all | solution.py:160
  18.4 7.6 %copy-start.6 = (bf16[12,14,14,256]{3,2,1,0:T(8,128)(2,1)S(1)}, bf16[12,14,14,256]{3,2,1,0:T(8,128)(2,1)}, u32[]{:S(2)}) copy-start(bf16[12,14,14,256]{3,2,1,0:T(8,128)(2,1)} %param.20) | copy-start | bytes 3612676
  20.6 192.3 %collective-permute-start.6 = (bf16[1,64,256]{2,0,1:T(2,128)(2,1)}, bf16[1,64,256]{2,0,1:T(2,128)(2,1)S(1)}, u32[]{:S(2)}, u32[]{:S(2)}) collective-permute-start(bf16[1,64,256]{2,0,1:T(2,128)(2,1)} %get-tuple-element.55), channel_id=1, source_target_pairs={{0,16},{16,32},{32,48},{48,64},{64,80},{80,96},{96,112},{1,17},{17... | collective-permute-start | bytes 98312 | tf_op jit(solution)/shard_map/ppermute | solution.py:18
  22.1 4.1 copy-start.2
  22.1 190.9 %collective-permute-start.7 = (bf16[1,64,256]{2,0,1:T(2,128)(2,1)S(1)}, bf16[1,64,256]{2,0,1:T(2,128)(2,1)S(1)}, u32[]{:S(2)}, u32[]{:S(2)}) collective-permute-start(bf16[1,64,256]{2,0,1:T(2,128)(2,1)S(1)} %get-tuple-element.56), channel_id=1, source_target_pairs={{16,0},{32,16},{48,32},{64,48},{80,64},{96,80},{112,96},{17,1},{33... | collective-permute-start | bytes 98312 | tf_op jit(solution)/shard_map/ppermute | solution.py:21
  97.3 2.7 copy-start.12
  97.3 3.9 copy-start.11
  99.9 2.4 copy-start.4
  118.0 2.6 copy-start.10
  118.0 3.8 copy-start.8
  120.6 2.4 copy-start.9
  121.8 2.4 copy-start.15
  145.1 1.3 copy-start.7
  156.6 7.3 %copy-start.3 = (bf16[12,14,14,256]{3,2,1,0:T(8,128)(2,1)S(1)}, bf16[12,14,14,256]{3,2,1,0:T(8,128)(2,1)}, u32[]{:S(2)}) copy-start(bf16[12,14,14,256]{3,2,1,0:T(8,128)(2,1)} %param.19) | copy-start | bytes 3612676
  156.6 70.4 %all-to-all-start.1 = ((bf16[16,2,16,16,256]{4,3,2,1,0:T(8,128)(2,1)}), bf16[16,2,16,16,256]{4,3,2,1,0:T(8,128)(2,1)}, u32[]{:S(2)}, u32[]{:S(2)}) async-start(bf16[16,2,16,16,256]{4,3,2,1,0:T(8,128)(2,1)} %bitcast.83), calls=%async_computation.1 | async-start | bytes 8388608 | tf_op jit(solution)/shard_map/all_to_all | solution.py:159
  163.9 292.5 %all-reduce.10.cloned.1.call-start = ((), (), s32[]{:S(2)}) async-start(), calls=%async_computation.2 | async-start | bytes 14155776
  184.0 16.8 %copy-start.5 = (bf16[2352,256]{1,0:T(8,128)(2,1)S(1)}, bf16[2352,256]{1,0:T(8,128)(2,1)}, u32[]{:S(2)}) copy-start(bf16[2352,256]{1,0:T(8,128)(2,1)} %fusion.2) | copy-start | bytes 3612676
  213.0 5.2 %collective-permute-start.8 = (bf16[18,1,256]{2,0,1:T(8,128)(2,1)S(1)}, bf16[18,1,256]{2,0,1:T(8,128)(2,1)S(1)}, u32[]{:S(2)}, u32[]{:S(2)}) collective-permute-start(bf16[18,1,256]{2,0,1:T(8,128)(2,1)S(1)} %get-tuple-element.50), channel_id=1, source_target_pairs={{0,1},{1,2},{2,3},{3,4},{4,5},{5,6},{6,7},{7,8},{8,9},{9,10},{10,1... | collective-permute-start | bytes 27656 | tf_op jit(solution)/shard_map/ppermute | solution.py:18
  216.8 5.6 %collective-permute-start.9 = (bf16[18,1,256]{2,0,1:T(8,128)(2,1)S(1)}, bf16[18,1,256]{2,0,1:T(8,128)(2,1)S(1)}, u32[]{:S(2)}, u32[]{:S(2)}) collective-permute-start(bf16[18,1,256]{2,0,1:T(8,128)(2,1)S(1)} %get-tuple-element.49), channel_id=1, source_target_pairs={{1,0},{2,1},{3,2},{4,3},{5,4},{6,5},{7,6},{8,7},{9,8},{10,9},{11,1... | collective-permute-start | bytes 27656 | tf_op jit(solution)/shard_map/ppermute | solution.py:21
  238.8 24.6 %copy-start.13 = (bf16[16,64,256]{2,1,0:T(8,128)(2,1)S(1)}, bf16[16,64,256]{2,1,0:T(8,128)(2,1)}, u32[]{:S(2)}) copy-start(bf16[16,64,256]{2,1,0:T(8,128)(2,1)} %param.29) | copy-start | bytes 1572868
  259.8 10.0 %collective-permute-start = (bf16[32,16,256]{2,0,1:T(8,128)(2,1)S(1)}, bf16[32,16,256]{2,0,1:T(8,128)(2,1)S(1)}, u32[]{:S(2)}, u32[]{:S(2)}) collective-permute-start(bf16[32,16,256]{2,0,1:T(8,128)(2,1)S(1)} %slice.393), channel_id=1, source_target_pairs={{0,1},{1,2},{2,3},{3,4},{4,5},{5,6},{6,7},{7,8},{8,9},{9,10},{10,1... | collective-permute-start | bytes 786440 | tf_op jit(solution)/shard_map/ppermute | solution.py:10
  269.8 5.5 %copy-start.16 = (bf16[16,64,256]{2,1,0:T(8,128)(2,1)S(1)}, bf16[16,64,256]{2,1,0:T(8,128)(2,1)}, u32[]{:S(2)}) copy-start(bf16[16,64,256]{2,1,0:T(8,128)(2,1)} %param.30) | copy-start | bytes 1572868
  269.9 5.4 %collective-permute-start.1 = (bf16[16,64,256]{2,0,1:T(8,128)(2,1)S(1)}, bf16[16,64,256]{2,0,1:T(8,128)(2,1)S(1)}, u32[]{:S(2)}, u32[]{:S(2)}) collective-permute-start(bf16[16,64,256]{2,0,1:T(8,128)(2,1)S(1)} %slice.392), channel_id=1, source_target_pairs={{0,16},{16,32},{32,48},{48,64},{64,80},{80,96},{96,112},{1,17},{17... | collective-permute-start | bytes 1572872 | tf_op jit(solution)/shard_map/ppermute | solution.py:10
  281.2 18.3 %copy-start.14 = (bf16[3,3,256,256]{3,2,1,0:T(8,128)(2,1)S(1)}, bf16[3,3,256,256]{3,2,1,0:T(8,128)(2,1)}, u32[]{:S(2)}) copy-start(bf16[3,3,256,256]{3,2,1,0:T(8,128)(2,1)} %param.31) | copy-start | bytes 3538948
  281.3 8.0 %collective-permute-start.2 = (bf16[1,64,256]{2,0,1:T(2,128)(2,1)S(1)}, bf16[1,64,256]{2,0,1:T(2,128)(2,1)S(1)}, u32[]{:S(2)}, u32[]{:S(2)}) collective-permute-start(bf16[1,64,256]{2,0,1:T(2,128)(2,1)S(1)} %get-tuple-element.57), channel_id=1, source_target_pairs={{0,16},{16,32},{32,48},{48,64},{64,80},{80,96},{96,112},{1,17},{17... | collective-permute-start | bytes 98312 | tf_op jit(solution)/shard_map/ppermute | solution.py:18
  288.0 5.1 %collective-permute-start.3 = (bf16[1,64,256]{2,0,1:T(2,128)(2,1)S(1)}, bf16[1,64,256]{2,0,1:T(2,128)(2,1)S(1)}, u32[]{:S(2)}, u32[]{:S(2)}) collective-permute-start(bf16[1,64,256]{2,0,1:T(2,128)(2,1)S(1)} %get-tuple-element.58), channel_id=1, source_target_pairs={{16,0},{32,16},{48,32},{64,48},{80,64},{96,80},{112,96},{17,1},{33... | collective-permute-start | bytes 98312 | tf_op jit(solution)/shard_map/ppermute | solution.py:21
  293.1 7.1 %collective-permute-start.4 = (bf16[18,1,256]{2,0,1:T(8,128)(2,1)S(1)}, bf16[18,1,256]{2,0,1:T(8,128)(2,1)S(1)}, u32[]{:S(2)}, u32[]{:S(2)}) collective-permute-start(bf16[18,1,256]{2,0,1:T(8,128)(2,1)S(1)} %get-tuple-element.54), channel_id=1, source_target_pairs={{1,0},{2,1},{3,2},{4,3},{5,4},{6,5},{7,6},{8,7},{9,8},{10,9},{11,1... | collective-permute-start | bytes 27656 | tf_op jit(solution)/shard_map/ppermute | solution.py:21
  294.4 6.4 %collective-permute-start.5 = (bf16[18,1,256]{2,0,1:T(8,128)(2,1)S(1)}, bf16[18,1,256]{2,0,1:T(8,128)(2,1)S(1)}, u32[]{:S(2)}, u32[]{:S(2)}) collective-permute-start(bf16[18,1,256]{2,0,1:T(8,128)(2,1)S(1)} %get-tuple-element.53), channel_id=1, source_target_pairs={{0,1},{1,2},{2,3},{3,4},{4,5},{5,6},{6,7},{7,8},{8,9},{9,10},{10,1... | collective-permute-start | bytes 27656 | tf_op jit(solution)/shard_map/ppermute | solution.py:18
  304.4 156.2 %copy-start.1 = (bf16[12,16,14]{2,1,0:T(8,128)(2,1)S(1)}, bf16[12,16,14]{2,1,0:T(8,128)(2,1)}, u32[]{:S(2)}) copy-start(bf16[12,16,14]{2,1,0:T(8,128)(2,1)} %param.24) | copy-start | bytes 16132
Sparse Core Ops, SparseCore 0:
  281.3 175.0 all-reduce.9
where the time goes:
time: 475 us; the launch traced here: 468 us
  waiting for transfers between devices  162 us (34%)
  local copies, waits for them, and re-layouts  161 us (34%)
  matrix products  76.4 us (16%)
  starting transfers between devices  43.3 us (9%)
  between operations  15 us (3%)
  other arithmetic  9.96 us (2%)
    unnamed x2, waiting for transfers between devices  150 us
    unnamed x87, local copies, waits for them, and re-layouts  63.9 us
    concatenate x15, local copies, waits for them, and re-layouts, window_patches(): return jnp.concatenate(pieces, axis=-1)  31.8 us
    dot_general x1, matrix products, place_windows(): jnp.einsum('sYy,syXc->YXc', row_hit, spread, preferred_element_type=jnp.f...  20.9 us
    dot_general x3, matrix products, weight_term(): lax.dot_general(gradient, inputs_patch, (((0,), (0,)), ((), ())), preferr...  18.1 us
    ppermute x4, starting transfers between devices, extended(): lax.ppermute(lax.slice_in_dim(block, block.shape[dim] - width, None, axis...  16.9 us
    reshape x1, local copies, waits for them, and re-layouts, local(): window_patches(jnp.pad(grad_two, region_pad), pool_size, pool_size, True)  16.8 us
    reshape x1, local copies, waits for them, and re-layouts, local(): window_patches(jnp.pad(roi_feat, region_pad), pool_size, pool_size, False)  16.7 us
  transfers between devices with their start and end apart: 13, of which 6 were waited for; matrix products, arithmetic and copies ran while one was open for 43% of the time, Pallas kernels for 0%

commit v1 on v0

v1 whole, which is shorter than its diff:
```python
import functools

import jax
import jax.numpy as jnp
from jax import lax
from jax.experimental import pallas as pl
from jax.experimental.pallas import tpu as pltpu
from jax.sharding import PartitionSpec as P

F32, BF = jnp.float32, jnp.bfloat16
MESH = pl.DeviceIdType.MESH
C = 256
NB, RB = 4, 256
M = NB * RB
TH, TW, PW = 16, 64, 80
FM = TH * PW
FROWS = 16 + 18 * PW + 16
GRP, GR = 32, 144
TN = (((0,), (0,)), ((), ()))
VM = pltpu.CompilerParams(vmem_limit_bytes=60 << 20)


def whole(shape, space=pltpu.VMEM):
    return pl.BlockSpec(memory_space=space)


def fixed(shape):
    zeros = (0,) * len(shape)
    return pl.BlockSpec(shape, lambda *_: zeros, pipeline_mode=pl.Buffered(1))


def load_padded(dst, src, fn=None):
    for r in range(NB):
        for y in range(14):
            v = src[r, y]
            dst[pl.ds(16 + r * RB + y * 16, 14), :] = v if fn is None else fn(v)


def spread(x3, v):
    n = v.shape[0]
    x3[:, 256:512] = v[...]
    x3[pl.ds(1, n - 1), 0:256] = v[pl.ds(0, n - 1), :]
    x3[pl.ds(0, n - 1), 512:768] = v[pl.ds(1, n - 1), :]


def flip_weights(wt, w):
    for dy in range(3):
        for kk in range(3):
            wt[dy, kk * C : (kk + 1) * C, :] = w[dy, 2 - kk].T


def conv_flipped(x3, wt, base, rows, pitch):
    acc = None
    for dy in range(3):
        t = jnp.dot(x3[pl.ds(base + (1 - dy) * pitch, rows), :], wt[dy], preferred_element_type=F32)
        acc = t if acc is None else acc + t
    return acc


def front_kernel(tgt, orow, ocol, pre_ref, g2_ref, w2_ref, w1_ref, rows_ref, cols_ref, win_ref, g1_ref, meta_ref, vb, x3, vp, wt2, wt1):
    step = pl.program_id(0)

    @pl.when(step == 0)
    def _():
        vb[...] = jnp.zeros_like(vb)
        vp[...] = jnp.zeros_like(vp)
        x3[...] = jnp.zeros_like(x3)
        meta_ref[...] = jnp.zeros_like(meta_ref)
        flip_weights(wt2, w2_ref)
        flip_weights(wt1, w1_ref)

    load_padded(vb, g2_ref)
    load_padded(vp, pre_ref)
    spread(x3, vb)
    b2 = conv_flipped(x3, wt2, 16, M, 16)
    g1 = jnp.where(vp[pl.ds(16, M), :] > 0, b2, 0.0).astype(BF)
    g1_ref[...] = g1.reshape(NB, RB, C)
    vb[pl.ds(16, M), :] = g1
    spread(x3, vb)
    rg = conv_flipped(x3, wt1, 16, M, 16).astype(BF)
    lane = lax.broadcasted_iota(jnp.int32, (14, 256), 1)
    bin_ = lax.broadcasted_iota(jnp.int32, (14, 256), 0)
    pick_row = (lax.shift_right_logical(lane, 4) == bin_).astype(BF)
    pick_col = ((lane & 15) == bin_).astype(BF)
    lanes = lax.broadcasted_iota(jnp.int32, (8, 128), 1)
    for r in range(NB):
        rl = jnp.dot(rows_ref[r], pick_row, preferred_element_type=F32)
        cl = jnp.dot(cols_ref[r], pick_col, preferred_element_type=F32)
        both = (rl[:, None, :] * cl[None, :, :]).reshape(256, 256).astype(BF)
        win = jnp.dot(both, rg[r * RB : (r + 1) * RB], preferred_element_type=F32)
        at = step * NB + r
        t = tgt[at]
        k = lax.fori_loop(0, at, lambda q, s: s + jnp.where(tgt[q] == t, 1, 0), 0)
        win_ref[t * 2 + k] = win.astype(BF)
        old = meta_ref[t]
        new = jnp.where(lanes == 4 * k, 1, old)
        new = jnp.where(lanes == 4 * k + 1, orow[at], new)
        meta_ref[t] = jnp.where(lanes == 4 * k + 2, ocol[at], new)


def front(tgt, orow, ocol, pre, g2, w2, w1, rows, cols):
    blk = pl.BlockSpec((NB, 14, 14, C), lambda i, *_: (i, 0, 0, 0))
    rspec = pl.BlockSpec((NB, 16, 14), lambda i, *_: (i, 0, 0))
    return pl.pallas_call(
        front_kernel,
        grid_spec=pltpu.PrefetchScalarGridSpec(
            num_scalar_prefetch=3,
            grid=(3,),
            in_specs=[blk, blk, fixed((3, 3, C, C)), fixed((3, 3, C, C)), rspec, rspec],
            out_specs=[fixed((32, 256, C)), pl.BlockSpec((NB, RB, C), lambda i, *_: (i, 0, 0)), fixed((16, 8, 128))],
            scratch_shapes=[
                pltpu.VMEM((M + 32, C), BF),
                pltpu.VMEM((M + 32, 3 * C), BF),
                pltpu.VMEM((M + 32, C), BF),
                pltpu.VMEM((3, 3 * C, C), BF),
                pltpu.VMEM((3, 3 * C, C), BF),
            ],
        ),
        out_shape=[
            jax.ShapeDtypeStruct((32, 256, C), BF),
            jax.ShapeDtypeStruct((12, RB, C), BF),
            jax.ShapeDtypeStruct((16, 8, 128), jnp.int32),
        ],
        compiler_params=VM,
        cost_estimate=pl.CostEstimate(flops=8 * 10**9, bytes_accessed=12 << 20, transcendentals=0),
        name="front",
    )(tgt, orow, ocol, pre, g2, w2, w1, rows, cols)


def emit_groups(acc, out, lead):
    for g in range(GRP):
        for j in range(9):
            lo = acc[g * 8 : (g + 1) * 8, j * 256 : j * 256 + 128]
            hi = acc[g * 8 : (g + 1) * 8, j * 256 + 128 : (j + 1) * 256]
            out[lead, g, j * 16 : (j + 1) * 16, :] = jnp.concatenate([lo, hi], axis=0).astype(BF)


def terms_kernel(g2_ref, pre_ref, feat_ref, g1_ref, t_ref, vb, vx, x3, acc2, acc1):
    step = pl.program_id(0)

    @pl.when(step == 0)
    def _():
        for b in (vb, vx, x3, acc2, acc1):
            b[...] = jnp.zeros_like(b)

    load_padded(vx, pre_ref, lambda v: jnp.maximum(v, 0))
    spread(x3, vx)
    load_padded(vb, g2_ref)
    gt = vb[pl.ds(16, M), :].T
    for dy in range(3):
        acc2[:, dy * 768 : (dy + 1) * 768] += jnp.dot(gt, x3[pl.ds(dy * 16, M), :], preferred_element_type=F32)
    load_padded(vx, feat_ref)
    spread(x3, vx)
    gt = g1_ref[...].reshape(M, C).T
    for dy in range(3):
        acc1[:, dy * 768 : (dy + 1) * 768] += jnp.dot(gt, x3[pl.ds(dy * 16, M), :], preferred_element_type=F32)

    @pl.when(step == 2)
    def _():
        emit_groups(acc1, t_ref, 0)
        emit_groups(acc2, t_ref, 1)


def terms(g2, pre, feat, g1):
    blk = pl.BlockSpec((NB, 14, 14, C), lambda i: (i, 0, 0, 0))
    return pl.pallas_call(
        terms_kernel,
        grid=(3,),
        in_specs=[blk, blk, blk, pl.BlockSpec((NB, RB, C), lambda i: (i, 0, 0))],
        out_specs=fixed((2, GRP, GR, 128)),
        scratch_shapes=[
            pltpu.VMEM((M + 32, C), BF),
            pltpu.VMEM((M + 32, C), BF),
            pltpu.VMEM((M + 32, 3 * C), BF),
            pltpu.VMEM((C, 9 * C), F32),
            pltpu.VMEM((C, 9 * C), F32),
        ],
        out_shape=jax.ShapeDtypeStruct((2, GRP, GR, 128), BF),
        compiler_params=VM,
        cost_estimate=pl.CostEstimate(flops=8 * 10**9, bytes_accessed=12 << 20, transcendentals=0),
        name="terms",
    )(g2, pre, feat, g1)


def place_kernel(meta, win_ref, own_ref, right_ref, down_ref, diag_ref, canvas):
    canvas[...] = jnp.zeros_like(canvas)

    def slot(s, carry):
        d, k = s // 2, s % 2

        @pl.when(meta[d, 0, 4 * k] == 1)
        def _():
            row, col = meta[d, 0, 4 * k + 1], meta[d, 0, 4 * k + 2]
            for y in range(16):
                w = win_ref[s, y * 16 : (y + 1) * 16, :].astype(F32)
                canvas[0, row + y, pl.ds(col, 16), :] += w[:, 0:128]
                canvas[1, row + y, pl.ds(col, 16), :] += w[:, 128:256]

        return carry

    lax.fori_loop(0, 32, slot, 0)
    for h in range(2):
        part = slice(h * 128, (h + 1) * 128)
        own_ref[:, :, part] = canvas[h, 0:TH, 0:TW, :]
        right_ref[:, :, part] = canvas[h, 0:TH, TW:PW, :].astype(BF)
        down_ref[:, :, part] = canvas[h, TH:, 0:TW, :].astype(BF)
        diag_ref[:, :, part] = canvas[h, TH:, TW:PW, :].astype(BF)


def place(meta, win):
    return pl.pallas_call(
        place_kernel,
        in_specs=[whole(None, pltpu.SMEM), whole(None)],
        out_specs=[whole(None)] * 4,
        out_shape=[
            jax.ShapeDtypeStruct((TH, TW, C), F32),
            jax.ShapeDtypeStruct((TH, 16, C), BF),
            jax.ShapeDtypeStruct((TH, TW, C), BF),
            jax.ShapeDtypeStruct((TH, 16, C), BF),
        ],
        scratch_shapes=[pltpu.VMEM((2, 2 * TH, PW, 128), F32)],
        compiler_params=VM,
        name="place",
    )(meta, win)


def position():
    return lax.axis_index("ty"), lax.axis_index("tx")


def greet(peers):
    barrier = pltpu.get_barrier_semaphore()
    for peer in peers:
        pl.semaphore_signal(barrier, inc=1, device_id=peer, device_id_type=MESH)
    pl.semaphore_wait(barrier, len(peers))


def remote(src, dst, send, recv, peer):
    return pltpu.make_async_remote_copy(src, dst, send, recv, device_id=peer, device_id_type=MESH)


AROUND = [(-1, -1), (-1, 0), (-1, 1), (0, -1), (0, 1), (1, -1), (1, 0), (1, 1)]


def tile_kernel(own, right, down, diag, grad, inp, fg_pad, in_pad, fg, cols_out, rows_in, cols_in, r_right, r_down, r_diag, ssem, rsem):
    ty, tx = position()
    peer = {(a, b): (lax.rem(ty + a + 8, 8), lax.rem(tx + b + 16, 16)) for a, b in AROUND}
    there = {(a, b): jnp.logical_and(
        (ty + a >= 0) & (ty + a < 8), (tx + b >= 0) & (tx + b < 16)) for a, b in AROUND}
    greet([peer[p] for p in AROUND])

    def halo(n, block):
        cols_out[n, 0] = block[:, 0, :]
        cols_out[n, 1] = block[:, TW - 1, :]
        copies = []
        for i, (a, b) in enumerate(AROUND):
            if b == 0:
                src = block.at[0 if a < 0 else TH - 1]
                dst = rows_in.at[n, 1 if a < 0 else 0]
            else:
                src = cols_out.at[n, 0 if b < 0 else 1]
                dst = cols_in.at[n, 7 - i]
            copies.append(remote(src, dst, ssem.at[n * 8 + i], rsem.at[n * 8 + 7 - i], peer[(a, b)]))
        for copy in copies:
            copy.start()
        return copies

    def build(n, block, pad):
        zero = jnp.zeros((16, C), F32)

        def column(a, b):
            i = AROUND.index((a, b))
            return jnp.where(there[(a, b)], cols_in[n, i].astype(F32), 0.0)

        low = [column(-1, -1), column(0, -1), column(1, -1)]
        high = [column(-1, 1), column(0, 1), column(1, 1)]
        at = lax.broadcasted_iota(jnp.int32, (16, C), 0)

        def edge(parts, y):
            v, r = (parts[0], 15) if y < 0 else (parts[2], 0) if y > 15 else (parts[1], y)
            return v[r : r + 1, :]

        for y in range(-2, 17):
            gap = zero
            if y >= -1:
                gap = jnp.where(at == 0, edge(high, y), gap)
            if y <= 15:
                gap = jnp.where(at == 15, edge(low, y + 1), gap)
            pad[pl.ds(16 + (y + 1) * PW + TW, 16), :] = gap.astype(BF)
        for k, a in ((0, -1), (1, 1)):
            row = jnp.where(there[(a, 0)], rows_in[n, k].astype(F32), 0.0).astype(BF)
            pad[pl.ds(16 + (0 if a < 0 else 17) * PW, TW), :] = row
        for y in range(TH):
            pad[pl.ds(16 + (y + 1) * PW, TW), :] = block[y]

    first = halo(0, inp)
    spill = [
        remote(right, r_right, ssem.at[16], rsem.at[16], peer[(0, 1)]),
        remote(down, r_down, ssem.at[17], rsem.at[17], peer[(1, 0)]),
        remote(diag, r_diag, ssem.at[18], rsem.at[18], peer[(1, 1)]),
    ]
    for copy in spill:
        copy.start()
    for copy in first:
        copy.wait()
    build(0, inp, in_pad)
    for copy in spill:
        copy.wait()
    for y in range(TH):
        total = grad[y].astype(F32) + own[y] + jnp.where(there[(-1, 0)], r_down[y].astype(F32), 0.0)
        side = jnp.where(there[(0, -1)], r_right[y].astype(F32), 0.0)
        side += jnp.where(there[(-1, -1)], r_diag[y].astype(F32), 0.0)
        fg[y, 0:16, :] = (total[0:16] + side).astype(BF)
        fg[y, 16:TW, :] = total[16:].astype(BF)
    second = halo(1, fg)
    for copy in second:
        copy.wait()
    build(1, fg, fg_pad)


def tile_exchange(own, right, down, diag, grad, inp):
    return pl.pallas_call(
        tile_kernel,
        in_specs=[whole(None)] * 6,
        out_specs=[whole(None)] * 2,
        out_shape=[jax.ShapeDtypeStruct((FROWS, C), BF)] * 2,
        scratch_shapes=[
            pltpu.VMEM((TH, TW, C), BF),
            pltpu.VMEM((2, 2, TH, C), BF),
            pltpu.VMEM((2, 2, TW, C), BF),
            pltpu.VMEM((2, 8, TH, C), BF),
            pltpu.VMEM((TH, 16, C), BF),
            pltpu.VMEM((TH, TW, C), BF),
            pltpu.VMEM((TH, 16, C), BF),
            pltpu.SemaphoreType.DMA((19,)),
            pltpu.SemaphoreType.DMA((19,)),
        ],
        compiler_params=pltpu.CompilerParams(vmem_limit_bytes=60 << 20, collective_id=1, has_side_effects=True),
        name="tile_exchange",
    )(own, right, down, diag, grad, inp)


def scatter_kernel(nt, with_meta, *refs):
    if with_meta:
        b, meta, out, meta_in, r0, a1, r1, a2, r2, a3, r3, total, ssem, rsem, msend, mrecv, mlocal = refs
    else:
        b, out, r0, a1, r1, a2, r2, a3, r3, total, ssem, rsem = refs
    ty, tx = position()
    x, c, y, z = ty // 2, ty % 2, tx // 4, tx % 4
    other = (x * 2 + 1 - c, tx)
    px = [(lax.rem(x + k, 4) * 2 + c, tx) for k in (1, 2, 3)]
    py = [(ty, lax.rem(y + k, 4) * 4 + z) for k in (1, 2, 3)]
    pz = [(ty, y * 4 + lax.rem(z + k, 4)) for k in (1, 2, 3)]
    row = [(ty, lax.rem(tx + k, 16)) for k in range(1, 16)]
    greet([other] + px + (row if with_meta else py + pz))
    first = remote(b.at[:, :, 1 - c], r0, ssem.at[0], rsem.at[0], other)
    first.start()
    letters = []
    if with_meta:
        for k in range(1, 16):
            letters.append(
                remote(meta.at[lax.rem(tx + k, 16)], meta_in.at[tx], msend.at[k - 1], mrecv.at[k - 1], row[k - 1])
            )
        for letter in letters:
            letter.start()
        keep = pltpu.make_async_copy(meta.at[tx], meta_in.at[tx], mlocal)
        keep.start()
    first.wait()
    for xx in range(4):
        a1[:, xx] = (b[:, xx, c].astype(F32) + r0[:, xx].astype(F32)).astype(BF)
    copies = [
        remote(a1.at[:, lax.rem(x + k, 4)], r1.at[k - 1], ssem.at[k], rsem.at[k], px[k - 1]) for k in (1, 2, 3)
    ]
    for copy in copies:
        copy.start()
    mine = a1[:, x].astype(F32)
    for copy in copies:
        copy.wait()
    a2[...] = (mine + r1[0].astype(F32) + r1[1].astype(F32) + r1[2].astype(F32)).astype(BF)
    copies = [
        remote(a2.at[:, lax.rem(y + k, 4)], r2.at[k - 1], ssem.at[3 + k], rsem.at[3 + k], py[k - 1]) for k in (1, 2, 3)
    ]
    for copy in copies:
        copy.start()
    mine = a2[:, y].astype(F32)
    for copy in copies:
        copy.wait()
    a3[...] = (mine + r2[0].astype(F32) + r2[1].astype(F32) + r2[2].astype(F32)).astype(BF)
    copies = [remote(a3, r3.at[k - 1], ssem.at[6 + k], rsem.at[6 + k], pz[k - 1]) for k in (1, 2, 3)]
    for copy in copies:
        copy.start()
    for copy in copies:
        copy.wait()
    total[...] = a3[...].astype(F32) + r3[0].astype(F32) + r3[1].astype(F32) + r3[2].astype(F32)
    for t in range(nt):
        for bit in range(2):
            out[t, bit * 18 : (bit + 1) * 18, :] = total[t, pl.ds(2 * z + bit, 18, stride=8), :]
    if with_meta:
        for letter in letters:
            letter.wait()
        keep.wait()


def scatter(parts, meta, cid):
    nt = parts.shape[0]
    shaped = parts.reshape(nt, 4, 2, 4, GR, 128)
    out_shape = [jax.ShapeDtypeStruct((nt, 36, 128), F32)]
    scratch = [
        pltpu.VMEM((nt, 4, 4, GR, 128), BF),
        pltpu.VMEM((nt, 4, 4, GR, 128), BF),
        pltpu.VMEM((3, nt, 4, GR, 128), BF),
        pltpu.VMEM((nt, 4, GR, 128), BF),
        pltpu.VMEM((3, nt, GR, 128), BF),
        pltpu.VMEM((nt, GR, 128), BF),
        pltpu.VMEM((3, nt, GR, 128), BF),
        pltpu.VMEM((nt, GR, 128), F32),
        pltpu.SemaphoreType.DMA((10,)),
        pltpu.SemaphoreType.DMA((10,)),
    ]
    operands = [shaped]
    if meta is not None:
        out_shape.append(jax.ShapeDtypeStruct((16, 8, 128), jnp.int32))
        scratch += [pltpu.SemaphoreType.DMA((15,)), pltpu.SemaphoreType.DMA((15,)), pltpu.SemaphoreType.DMA(())]
        operands.append(meta)
    return pl.pallas_call(
        functools.partial(scatter_kernel, nt, meta is not None),
        in_specs=[whole(None)] * len(operands),
        out_specs=[whole(None)] * len(out_shape),
        out_shape=out_shape,
        scratch_shapes=scratch,
        compiler_params=pltpu.CompilerParams(vmem_limit_bytes=60 << 20, collective_id=cid, has_side_effects=True),
        cost_estimate=pl.CostEstimate(flops=10**9, bytes_accessed=16 << 20, transcendentals=0),
        name="scatter",
    )(*operands)


def tile_conv_kernel(fg_pad, in_pad, w_ref, out, t_ref, x3, wt, acc):
    flip_weights(wt, w_ref)
    n = FROWS
    x3[0:16, :] = jnp.zeros((16, 3 * C), BF)
    x3[n - 16 :, :] = jnp.zeros((16, 3 * C), BF)
    spread(x3, fg_pad)
    res = conv_flipped(x3, wt, 16 + PW, FM, PW).astype(BF).reshape(TH, PW, C)
    out[...] = res[:, 0:TW, :]
    at = lax.broadcasted_iota(jnp.int32, (TH, PW, C), 1).reshape(FM, C)
    g = jnp.where(at < TW, fg_pad[pl.ds(16 + PW, FM), :].astype(F32), 0.0).astype(BF)
    gt = g.T
    spread(x3, in_pad)
    for dy in range(3):
        acc[:, dy * 768 : (dy + 1) * 768] = jnp.dot(gt, x3[pl.ds(16 + dy * PW, FM), :], preferred_element_type=F32)
    emit_groups(acc, t_ref, 0)


def tile_conv(fg_pad, in_pad, w):
    return pl.pallas_call(
        tile_conv_kernel,
        in_specs=[whole(None)] * 3,
        out_specs=[whole(None)] * 2,
        out_shape=[jax.ShapeDtypeStruct((TH, TW, C), BF), jax.ShapeDtypeStruct((1, GRP, GR, 128), BF)],
        scratch_shapes=[
            pltpu.VMEM((FROWS, 3 * C), BF),
            pltpu.VMEM((3, 3 * C, C), BF),
            pltpu.VMEM((C, 9 * C), F32),
        ],
        compiler_params=VM,
        name="tile_conv",
    )(fg_pad, in_pad, w)


def local(roi_feat, pre_one, grad_two, w_one, w_two, roi_rows, roi_cols, target_col, off_row, off_col, fpn_input, fpn_grad, w_fpn):
    win, g1, meta = front(target_col[:, 0], off_row, off_col, pre_one, grad_two, w_two, w_one, roi_rows, roi_cols)
    win_in = lax.all_to_all(win.reshape(16, 512, C), "tx", split_axis=0, concat_axis=0, tiled=True)
    parts = terms(grad_two, pre_one, roi_feat, g1)
    heads, meta_in = scatter(parts, meta, 2)
    own, right, down, diag = place(meta_in, win_in.reshape(32, 256, C))
    fg_pad, in_pad = tile_exchange(own, right, down, diag, fpn_grad, fpn_input)
    grad_in, part = tile_conv(fg_pad, in_pad, w_fpn)
    (tail,) = scatter(part, None, 3)
    return grad_in, heads[0].reshape(-1), heads[1].reshape(-1), tail[0].reshape(-1)


def solution(mesh):
    both = ("ty", "tx")
    placed = (
        P(both, None, None, None),
        P(both, None, None, None),
        P(both, None, None, None),
        P(),
        P(),
        P(both, None, None),
        P(both, None, None),
        P(both, None),
        P(both),
        P(both),
        P("ty", "tx", None),
        P("ty", "tx", None),
        P(),
    )
    return jax.shard_map(
        local,
        mesh=mesh,
        in_specs=placed,
        out_specs=(P("ty", "tx", None), P(both), P(both), P(both)),
        check_vma=False,
    )
```

time: 475 us -> 169 us (0.36); the launches traced: 468 us -> 168 us
  waiting for transfers between devices: 162 us -> 0.01 us
  local copies, waits for them, and re-layouts: 161 us -> 2.7 us
  Pallas kernels: 0 us -> 157 us
  matrix products: 76.4 us -> 0 us
  starting transfers between devices: 43.3 us -> 8.23 us
  between operations: 15 us -> 0.67 us
  other arithmetic: 9.96 us -> 0 us
    pallas_call x0 -> x7, Pallas kernels: none -> 157 us  [the longest x2 82.8 us: scatter(): pl.pallas_call(functools.partial(scatter_kernel, nt, meta is not None), i...]
    unnamed x2 -> x0, waiting for transfers between devices: 150 us -> none
    dot_general x12 -> x0, matrix products: 76.4 us -> none  [the longest x1 20.9 us: place_windows(): jnp.einsum('sYy,syXc->YXc', row_hit, spread, preferred_element_type=jnp.f...]
    unnamed x87 -> x1, local copies, waits for them, and re-layouts: 63.9 us -> 1.34 us
    reshape x9 -> x0, local copies, waits for them, and re-layouts: 48.5 us -> none  [the longest x1 16.8 us: local(): window_patches(jnp.pad(grad_two, region_pad), pool_size, pool_size, True)]
    concatenate x15 -> x0, local copies, waits for them, and re-layouts: 31.8 us -> none  [window_patches(): return jnp.concatenate(pieces, axis=-1)]
    ppermute x10 -> x0, starting transfers between devices: 27.9 us -> none  [the longest x4 16.9 us: extended(): lax.ppermute(lax.slice_in_dim(block, block.shape[dim] - width, None, axis...]
    ppermute x10 -> x0, waiting for transfers between devices: 12.6 us -> none  [the longest x4 8.03 us: extended(): lax.ppermute(lax.slice_in_dim(block, 0, width, axis=dim), axis, backward)]
  transfers between devices with their start and end apart: 13 -> 1, of which waited for: 6 -> 0; matrix products, arithmetic and copies ran while one was open for 43% -> 1% of each run, Pallas kernels for 0% -> 41%
where the time goes in v1:
time: 169 us; the launch traced here: 168 us
  Pallas kernels  157 us (93%)
  starting transfers between devices  8.23 us (5%)
  local copies, waits for them, and re-layouts  2.7 us (2%)
    pallas_call x2, Pallas kernels, scatter(): pl.pallas_call(functools.partial(scatter_kernel, nt, meta is not None), i...  82.8 us
    pallas_call x1, Pallas kernels, tile_exchange(): pl.pallas_call(tile_kernel, in_specs=[whole(None)] * 6, out_specs=[whole(...  26.1 us
    pallas_call x1, Pallas kernels, front(): pl.pallas_call(front_kernel, grid_spec=pltpu.PrefetchScalarGridSpec(num_s...  24.5 us
    pallas_call x1, Pallas kernels, terms(): pl.pallas_call(terms_kernel, grid=(3,), in_specs=[blk, blk, blk, pl.Block...  11.9 us
    all_to_all x1, starting transfers between devices, local(): lax.all_to_all(win.reshape(16, 512, C), 'tx', split_axis=0, concat_axis=0...  8.23 us
    pallas_call x1, Pallas kernels, tile_conv(): pl.pallas_call(tile_conv_kernel, in_specs=[whole(None)] * 3, out_specs=[w...  6.22 us
    pallas_call x1, Pallas kernels, place(): pl.pallas_call(place_kernel, in_specs=[whole(None, pltpu.SMEM), whole(Non...  5.2 us
  transfers between devices with their start and end apart: 1, of which 0 were waited for; matrix products, arithmetic and copies ran while one was open for 1% of the time, Pallas kernels for 41%

profile of v1, /device:TPU:0, one launch (start us, length us, event | category | flops | bytes accessed | tf_op | source)
XLA Modules:
  0.0 168.3 jit_solution(14189800626500450016)
XLA Ops:
  0.6 24.5 %front.1 = (bf16[32,256,256]{2,1,0:T(8,128)(2,1)}, bf16[12,256,256]{2,1,0:T(8,128)(2,1)}, s32[16,8,128]{2,1,0:T(8,128)}) custom-call(s32[12]{0:T(128)} %bitcast.13, s32[12]{0:T(128)} %orow.1, s32[12]{0:T(128)} %ocol.1, bf16[12,14,14,256]{3,2,1,0:T(8,128)(2,1)} %pre_ref.3, bf16[12,14,14,256]{3,2,1,0:T(8,128)(2,1)} %g2_ref.3, bf16[3,3,256,256]{3,2,1,0:T(8,128)(2,1)} %w2_ref.1, ...), custom_call_target="tpu_custom_call" | custom-call | flops 8000000000 | bytes 12582912 | tf_op jit(solution)/shard_map/front/pallas_call | solution.py:104
  25.1 8.2 %all-to-all-start = ((bf16[16,512,256]{2,1,0:T(8,128)(2,1)}), bf16[16,512,256]{2,1,0:T(8,128)(2,1)}, u32[]{:S(2)}, u32[]{:S(2)}) async-start(bf16[16,512,256]{2,1,0:T(8,128)(2,1)} %bitcast.10), calls=%async_computation | async-start | bytes 8388608 | tf_op jit(solution)/shard_map/all_to_all | solution.py:472
  33.4 11.9 %terms.1 = bf16[2,32,144,128]{3,2,1,0:T(8,128)(2,1)} custom-call(bf16[12,14,14,256]{3,2,1,0:T(8,128)(2,1)} %g2_ref.3, bf16[12,14,14,256]{3,2,1,0:T(8,128)(2,1)} %pre_ref.3, bf16[12,14,14,256]{3,2,1,0:T(8,128)(2,1)} %feat_ref.1, bf16[12,256,256]{2,1,0:T(8,128)(2,1)} %get-tuple-element.17.g1_ref), custom_call_target="tpu_custom_call" | custom-call | flops 8000000000 | bytes 12582912 | tf_op jit(solution)/shard_map/terms/pallas_call | solution.py:166
  45.3 57.0 %scatter.2 = (f32[2,36,128]{2,1,0:T(8,128)}, s32[16,8,128]{2,1,0:T(8,128)}) custom-call(bf16[2,4,2,4,144,128]{5,4,3,2,1,0:T(8,128)(2,1)} %bitcast.14, s32[16,8,128]{2,1,0:T(8,128)} %get-tuple-element.18.refs_1_), custom_call_target="tpu_custom_call" | custom-call | flops 1000000000 | bytes 16777216 | tf_op jit(solution)/shard_map/scatter/pallas_call | solution.py:425
  102.3 1.4 slice_bitcast_fusion
  103.6 0.0 all-to-all-done
  103.7 5.2 %place.1 = (f32[16,64,256]{2,1,0:T(8,128)}, bf16[16,16,256]{2,1,0:T(8,128)(2,1)}, bf16[16,64,256]{2,1,0:T(8,128)(2,1)}, bf16[16,16,256]{2,1,0:T(8,128)(2,1)}) custom-call(s32[16,8,128]{2,1,0:T(8,128)} %get-tuple-element.19.meta, bf16[32,256,256]{2,1,0:T(8,128)(2,1)} %bitcast.3.win_ref), custom_call_target="tpu_custom_call" | custom-call | tf_op jit(solution)/shard_map/place/pallas_call | solution.py:211
  108.9 26.1 %tile_exchange.1 = (bf16[1472,256]{1,0:T(8,128)(2,1)}, bf16[1472,256]{1,0:T(8,128)(2,1)}) custom-call(f32[16,64,256]{2,1,0:T(8,128)} %get-tuple-element.21.own, bf16[16,16,256]{2,1,0:T(8,128)(2,1)} %get-tuple-element.22.right, bf16[16,64,256]{2,1,0:T(8,128)(2,1)} %get-tuple-element.23.down, bf16[16,16,256]{2,1,0:T(8,128)(2,1)} %get-tuple-element.24.diag, ...), custom_call_target="tpu_custom_call" | custom-call | tf_op jit(solution)/shard_map/tile_exchange/pallas_call | solution.py:322
  135.0 6.2 %tile_conv.1 = (bf16[16,64,256]{2,1,0:T(8,128)(2,1)}, bf16[1,32,144,128]{3,2,1,0:T(8,128)(2,1)}) custom-call(bf16[1472,256]{1,0:T(8,128)(2,1)} %get-tuple-element.25.fg_pad, bf16[1472,256]{1,0:T(8,128)(2,1)} %get-tuple-element.26.in_pad, bf16[3,3,256,256]{3,2,1,0:T(8,128)(2,1)} %w_ref.1), custom_call_target="tpu_custom_call" | custom-call | tf_op jit(solution)/shard_map/tile_conv/pallas_call | solution.py:455
  141.2 25.8 %scatter.3 = f32[1,36,128]{2,1,0:T(8,128)} custom-call(bf16[1,4,2,4,144,128]{5,4,3,2,1,0:T(8,128)(2,1)} %bitcast.12), custom_call_target="tpu_custom_call" | custom-call | flops 1000000000 | bytes 16777216 | tf_op jit(solution)/shard_map/scatter/pallas_call | solution.py:425
  167.0 1.3 copy.18
Async XLA Ops:
  25.1 78.5 %all-to-all-start = ((bf16[16,512,256]{2,1,0:T(8,128)(2,1)}), bf16[16,512,256]{2,1,0:T(8,128)(2,1)}, u32[]{:S(2)}, u32[]{:S(2)}) async-start(bf16[16,512,256]{2,1,0:T(8,128)(2,1)} %bitcast.10), calls=%async_computation | async-start | bytes 8388608 | tf_op jit(solution)/shard_map/all_to_all | solution.py:472

commit v2 on v1

v2 whole, which is shorter than its diff:
```python
import jax
import jax.numpy as jnp
from jax import lax
from jax.experimental import pallas as pl
from jax.experimental.pallas import tpu as pltpu
from jax.sharding import PartitionSpec as P

F32, BF = jnp.float32, jnp.bfloat16
MESH = pl.DeviceIdType.MESH
C = 256
NB, RB = 4, 240
SR = 200
M = NB * RB
TH, TW, PW = 16, 64, 80
FM = TH * PW
FROWS = 16 + 18 * PW + 16
GR = 144
VM = pltpu.CompilerParams(vmem_limit_bytes=60 << 20)


def whole(shape, space=pltpu.VMEM):
    return pl.BlockSpec(memory_space=space)


def fixed(shape):
    zeros = (0,) * len(shape)
    return pl.BlockSpec(shape, lambda *_: zeros, pipeline_mode=pl.Buffered(1))


def load_padded(dst, src, fn=None, first=0):
    for r in range(NB):
        for y in range(14):
            v = src[first + r, y]
            dst[pl.ds(16 + r * RB + y * 16, 14), :] = v if fn is None else fn(v)


def spread(x3, v):
    n = v.shape[0]
    x3[:, 256:512] = v[...]
    x3[pl.ds(1, n - 1), 0:256] = v[pl.ds(0, n - 1), :]
    x3[pl.ds(0, n - 1), 512:768] = v[pl.ds(1, n - 1), :]


def flip_weights(wt, w):
    for dy in range(3):
        for kk in range(3):
            wt[dy, kk * C : (kk + 1) * C, :] = w[dy, 2 - kk].T


def conv_flipped(x3, wt, base, rows, pitch):
    acc = None
    for dy in range(3):
        t = jnp.dot(x3[pl.ds(base + (1 - dy) * pitch, rows), :], wt[dy], preferred_element_type=F32)
        acc = t if acc is None else acc + t
    return acc


def front_kernel(tgt, orow, ocol, pre_ref, g2_ref, w2_ref, w1_ref, rows_ref, cols_ref, slot_ref, g1_ref, meta_ref, wts_ref, vb, x3, vp, wt2, wt1):
    step = pl.program_id(0)

    @pl.when(step == 0)
    def _():
        vb[...] = jnp.zeros_like(vb)
        vp[...] = jnp.zeros_like(vp)
        x3[0:16] = jnp.zeros((16, 3 * C), BF)
        x3[M + 16 :] = jnp.zeros((16, 3 * C), BF)
        meta_ref[...] = jnp.zeros_like(meta_ref)
        wts_ref[...] = jnp.zeros_like(wts_ref)
        flip_weights(wt2, w2_ref)
        flip_weights(wt1, w1_ref)

    load_padded(vb, g2_ref)
    load_padded(vp, pre_ref)
    spread(x3, vb)
    b2 = conv_flipped(x3, wt2, 16, M, 16)
    g1 = jnp.where(vp[pl.ds(16, M), :] > 0, b2, 0.0).astype(BF)
    g1_ref[...] = g1.reshape(NB, RB, C)
    vb[pl.ds(16, M), :] = g1
    spread(x3, vb)
    rg = conv_flipped(x3, wt1, 16, M, 16).astype(BF)
    lanes = lax.broadcasted_iota(jnp.int32, (8, 128), 1)
    for r in range(NB):
        at = step * NB + r
        t = tgt[at]
        k = lax.fori_loop(0, at, lambda q, s: s + jnp.where(tgt[q] == t, 1, 0), 0)
        for i in range(14):
            slot_ref[t, k, pl.ds(i * 14, 14), :] = rg[r * RB + i * 16 : r * RB + i * 16 + 14]
        old = meta_ref[t]
        new = jnp.where(lanes == 4 * k, 1, old)
        new = jnp.where(lanes == 4 * k + 1, orow[at], new)
        meta_ref[t] = jnp.where(lanes == 4 * k + 2, ocol[at], new)
        wts_ref[t, k, :, 0:14] = rows_ref[r]
        wts_ref[t, k, :, 16:30] = cols_ref[r]


def front(tgt, orow, ocol, pre, g2, w2, w1, rows, cols):
    blk = pl.BlockSpec((NB, 14, 14, C), lambda i, *_: (i, 0, 0, 0))
    rspec = pl.BlockSpec((NB, 16, 14), lambda i, *_: (i, 0, 0))
    return pl.pallas_call(
        front_kernel,
        grid_spec=pltpu.PrefetchScalarGridSpec(
            num_scalar_prefetch=3,
            grid=(3,),
            in_specs=[blk, blk, fixed((3, 3, C, C)), fixed((3, 3, C, C)), rspec, rspec],
            out_specs=[
                fixed((16, 2, SR, C)),
                pl.BlockSpec((NB, RB, C), lambda i, *_: (i, 0, 0)),
                fixed((16, 8, 128)),
                fixed((16, 2, 16, 128)),
            ],
            scratch_shapes=[
                pltpu.VMEM((M + 32, C), BF),
                pltpu.VMEM((M + 32, 3 * C), BF),
                pltpu.VMEM((M + 32, C), BF),
                pltpu.VMEM((3, 3 * C, C), BF),
                pltpu.VMEM((3, 3 * C, C), BF),
            ],
        ),
        out_shape=[
            jax.ShapeDtypeStruct((16, 2, SR, C), BF),
            jax.ShapeDtypeStruct((12, RB, C), BF),
            jax.ShapeDtypeStruct((16, 8, 128), jnp.int32),
            jax.ShapeDtypeStruct((16, 2, 16, 128), BF),
        ],
        compiler_params=VM,
        cost_estimate=pl.CostEstimate(flops=8 * 10**9, bytes_accessed=12 << 20, transcendentals=0),
        name="front",
    )(tgt, orow, ocol, pre, g2, w2, w1, rows, cols)


def emit_groups(value, out, lead):
    for g in range(32):
        for j in range(value.shape[1] // 256):
            lo = value[g * 8 : (g + 1) * 8, j * 256 : j * 256 + 128]
            hi = value[g * 8 : (g + 1) * 8, j * 256 + 128 : (j + 1) * 256]
            both = jnp.concatenate([lo, hi], axis=0).astype(BF)
            out[lead, g // 8, g // 4 % 2, g % 4, j * 16 : (j + 1) * 16, :] = both


def place_kernel(meta, slots, wts, grad, own, p_down, p_right, p_diag, kcol, row0, canvas, rl, cl):
    canvas[...] = jnp.zeros_like(canvas)
    lane = lax.broadcasted_iota(jnp.int32, (128, 256), 1)
    at = lax.broadcasted_iota(jnp.int32, (128, 256), 0)
    i = lane // 14
    j = lane - i * 14
    used = lane < 196
    w = wts[...]
    rl[...] = jnp.dot(w, (used & (i == at)).astype(BF), preferred_element_type=F32).reshape(32, 16, 256)
    cl[...] = jnp.dot(w, (used & (j + 16 == at)).astype(BF), preferred_element_type=F32).reshape(32, 16, 256)
    for h in range(2):
        canvas[h, 0:TH, 0:TW, :] = grad[:, :, h * 128 : (h + 1) * 128].astype(F32)

    def slot(s, carry):
        d, k = s // 2, s % 2

        @pl.when(meta[d, 0, 4 * k] == 1)
        def _():
            row, col = meta[d, 0, 4 * k + 1], meta[d, 0, 4 * k + 2]
            both = (rl[s][:, None, :] * cl[s][None, :, :]).reshape(256, 256).astype(BF)
            win = jnp.dot(both[:, 0:196], slots[d, k, 0:196, :], preferred_element_type=F32)
            for y in range(16):
                for h in range(2):
                    canvas[h, row + y, pl.ds(col, 16), :] += win[y * 16 : (y + 1) * 16, h * 128 : (h + 1) * 128]

        return carry

    lax.fori_loop(0, 32, slot, 0)
    for h in range(2):
        part = slice(h * 128, (h + 1) * 128)
        own[:, :, part] = canvas[h, 0 : TH + 1, 0:TW, :]
        p_down[:, :, part] = canvas[h, TH - 1 : 31, 0:TW, :].astype(BF)
        p_right[:, :, part] = canvas[h, 0 : TH + 1, TW:PW, :].astype(BF)
        p_diag[:, :, part] = canvas[h, TH - 1 : 31, TW:PW, :].astype(BF)
        for n, col in enumerate((0, TW - 1, TW)):
            kcol[n, :, part] = canvas[h, :, col, :].astype(BF)
        row0[:, part] = canvas[h, 0, 0:TW, :].astype(BF)


def place(meta, slots, wts, grad):
    return pl.pallas_call(
        place_kernel,
        in_specs=[whole(None, pltpu.SMEM)] + [whole(None)] * 3,
        out_specs=[whole(None)] * 6,
        out_shape=[
            jax.ShapeDtypeStruct((TH + 1, TW, C), F32),
            jax.ShapeDtypeStruct((TH, TW, C), BF),
            jax.ShapeDtypeStruct((TH + 1, 16, C), BF),
            jax.ShapeDtypeStruct((TH, 16, C), BF),
            jax.ShapeDtypeStruct((3, 32, C), BF),
            jax.ShapeDtypeStruct((TW, C), BF),
        ],
        scratch_shapes=[
            pltpu.VMEM((2, 2 * TH, PW, 128), F32),
            pltpu.VMEM((32, 16, 256), F32),
            pltpu.VMEM((32, 16, 256), F32),
        ],
        compiler_params=VM,
        name="place",
    )(meta, slots, wts, grad)


def position():
    return lax.axis_index("ty"), lax.axis_index("tx")


def greet(peers):
    barrier = pltpu.get_barrier_semaphore()
    for peer in peers:
        pl.semaphore_signal(barrier, inc=1, device_id=peer, device_id_type=MESH)
    pl.semaphore_wait(barrier, len(peers))


def remote(src, dst, send, recv, peer):
    return pltpu.make_async_remote_copy(src, dst, send, recv, device_id=peer, device_id_type=MESH)


def go(copies):
    for copy in copies:
        copy.start()
    return copies


def settle(copies):
    for copy in copies:
        copy.wait()


def summed(mine, got):
    return mine.astype(F32) + got[0].astype(F32) + got[1].astype(F32) + got[2].astype(F32)


AROUND = [(-1, -1), (-1, 0), (-1, 1), (0, -1), (0, 1), (1, -1), (1, 0), (1, 1)]
ROW = [(0, 1), (1, 0), (0, 3), (3, 0), (1, 1), (3, 3), (1, 3), (3, 1), (0, 2), (2, 0), (1, 2), (2, 1), (3, 2), (2, 3), (2, 2)]


def around(ty, tx):
    peer = {(a, b): (lax.rem(ty + a + 8, 8), lax.rem(tx + b + 16, 16)) for a, b in AROUND}
    there = {
        (a, b): (ty + a >= 0) & (ty + a < 8) & (tx + b >= 0) & (tx + b < 16) for a, b in AROUND
    }
    return peer, there


def axes(ty, tx):
    x, c, y, z = ty // 2, ty % 2, tx // 4, tx % 4
    other = (x * 2 + 1 - c, tx)
    px = [(lax.rem(x + k, 4) * 2 + c, tx) for k in (1, 2, 3)]
    py = [(ty, lax.rem(y + k, 4) * 4 + z) for k in (1, 2, 3)]
    pz = [(ty, y * 4 + lax.rem(z + k, 4)) for k in (1, 2, 3)]
    return x, c, y, z, other, px, py, pz


def pad_input(block, pad, rows_in, cols_in, there):
    zero = jnp.zeros((16, C), F32)
    at = lax.broadcasted_iota(jnp.int32, (16, C), 0)

    def column(a, b):
        return jnp.where(there[(a, b)], cols_in[AROUND.index((a, b))].astype(F32), 0.0)

    low = [column(-1, -1), column(0, -1), column(1, -1)]
    high = [column(-1, 1), column(0, 1), column(1, 1)]

    def edge(parts, y):
        v, r = (parts[0], 15) if y < 0 else (parts[2], 0) if y > 15 else (parts[1], y)
        return v[r : r + 1, :]

    for y in range(-2, 17):
        gap = zero
        if y >= -1:
            gap = jnp.where(at == 0, edge(high, y), gap)
        if y <= 15:
            gap = jnp.where(at == 15, edge(low, y + 1), gap)
        pad[pl.ds(16 + (y + 1) * PW + TW, 16), :] = gap.astype(BF)
    pad[FROWS - 16 :, :] = jnp.zeros((16, C), BF)
    for k, a in ((0, -1), (1, 1)):
        row = jnp.where(there[(a, 0)], rows_in[k].astype(F32), 0.0).astype(BF)
        pad[pl.ds(16 + (0 if a < 0 else 17) * PW, TW), :] = row
    for y in range(TH):
        pad[pl.ds(16 + (y + 1) * PW, TW), :] = block[y]


def middle_kernel(
    slots, meta, wts, g2, pre, feat, g1, inp, slots_in, meta_in, wts_in, half, in_pad,
    vg2, vpre, vfeat, vg1, vb, vx, x3, acc2, acc1, parts, r0, a1, r1, cols_out, rows_in, cols_in,
    asend, arecv, msend, mrecv, wsend, wrecv, hsend, hrecv, ssend, srecv, keep, fetch,
):
    ty, tx = position()
    peer, there = around(ty, tx)
    x, c, y, z, other, px, _, _ = axes(ty, tx)
    row = [lax.rem(y + dy, 4) * 4 + lax.rem(z + dz, 4) for dy, dz in ROW]
    loads = go([pltpu.make_async_copy(s, d, fetch.at[i]) for i, (s, d) in enumerate(
        ((pre, vpre), (g2, vg2), (feat, vfeat), (g1, vg1)))])
    cols_out[0] = inp[:, 0, :]
    cols_out[1] = inp[:, TW - 1, :]
    greet([peer[p] for p in AROUND] + [(ty, q) for q in row] + [other] + px)
    letters = go([remote(meta.at[q], meta_in.at[tx], msend.at[i], mrecv.at[i], (ty, q)) for i, q in enumerate(row)])
    letters += go([remote(wts.at[q], wts_in.at[tx], wsend.at[i], wrecv.at[i], (ty, q)) for i, q in enumerate(row)])
    halo = []
    for i, (a, b) in enumerate(AROUND):
        if b == 0:
            src, dst = inp.at[0 if a < 0 else TH - 1], rows_in.at[1 if a < 0 else 0]
        else:
            src, dst = cols_out.at[0 if b < 0 else 1], cols_in.at[7 - i]
        halo.append(remote(src, dst, hsend.at[i], hrecv.at[7 - i], peer[(a, b)]))
    go(halo)
    sent = go([remote(slots.at[q], slots_in.at[tx], asend.at[i], arecv.at[i], (ty, q)) for i, q in enumerate(row)])
    kept = go([
        pltpu.make_async_copy(slots.at[tx], slots_in.at[tx], keep.at[0]),
        pltpu.make_async_copy(meta.at[tx], meta_in.at[tx], keep.at[1]),
        pltpu.make_async_copy(wts.at[tx], wts_in.at[tx], keep.at[2]),
    ])
    for b in (vb, vx, acc2, acc1):
        b[...] = jnp.zeros_like(b)
    x3[0:16] = jnp.zeros((16, 3 * C), BF)
    x3[M + 16 :] = jnp.zeros((16, 3 * C), BF)
    settle(loads)

    def step(n, carry):
        load_padded(vx, vpre, lambda v: jnp.maximum(v, 0), n * NB)
        spread(x3, vx)
        load_padded(vb, vg2, None, n * NB)
        gt = vb[pl.ds(16, M), :].T
        for dy in range(3):
            acc2[:, dy * 768 : (dy + 1) * 768] += jnp.dot(gt, x3[pl.ds(dy * 16, M), :], preferred_element_type=F32)
        load_padded(vx, vfeat, None, n * NB)
        spread(x3, vx)
        gt = vg1[pl.ds(n * NB, NB)].reshape(M, C).T
        for dy in range(3):
            acc1[:, dy * 768 : (dy + 1) * 768] += jnp.dot(gt, x3[pl.ds(dy * 16, M), :], preferred_element_type=F32)
        return carry

    lax.fori_loop(0, 3, step, 0)
    emit_groups(acc1, parts, 0)
    emit_groups(acc2, parts, 1)
    swap = go([remote(parts.at[:, :, 1 - c], r0, ssend.at[0], srecv.at[0], other)])
    settle(halo)
    pad_input(inp, in_pad, rows_in, cols_in, there)
    settle(swap)
    for xx in range(4):
        a1[:, xx] = (parts[:, xx, c].astype(F32) + r0[:, xx].astype(F32)).astype(BF)
    cross = go([remote(a1.at[:, lax.rem(x + k, 4)], r1.at[k - 1], ssend.at[k], srecv.at[k], px[k - 1]) for k in (1, 2, 3)])
    settle(cross)
    half[...] = summed(a1[:, x], r1).astype(BF)
    settle(letters)
    settle(sent)
    settle(kept)


def middle(slots, meta, wts, g2, pre, feat, g1, inp):
    hbm = whole(None, pltpu.HBM)
    vm = whole(None)
    dma = pltpu.SemaphoreType.DMA
    return pl.pallas_call(
        middle_kernel,
        in_specs=[hbm, vm, vm, hbm, hbm, hbm, hbm, vm],
        out_specs=[hbm, vm, vm, vm, vm],
        out_shape=[
            jax.ShapeDtypeStruct((16, 2, SR, C), BF),
            jax.ShapeDtypeStruct((16, 8, 128), jnp.int32),
            jax.ShapeDtypeStruct((16, 2, 16, 128), BF),
            jax.ShapeDtypeStruct((2, 4, GR, 128), BF),
            jax.ShapeDtypeStruct((FROWS, C), BF),
        ],
        scratch_shapes=[
            pltpu.VMEM((12, 14, 14, C), BF),
            pltpu.VMEM((12, 14, 14, C), BF),
            pltpu.VMEM((12, 14, 14, C), BF),
            pltpu.VMEM((12, RB, C), BF),
            pltpu.VMEM((M + 32, C), BF),
            pltpu.VMEM((M + 32, C), BF),
            pltpu.VMEM((M + 32, 3 * C), BF),
            pltpu.VMEM((C, 9 * C), F32),
            pltpu.VMEM((C, 9 * C), F32),
            pltpu.VMEM((2, 4, 2, 4, GR, 128), BF),
            pltpu.VMEM((2, 4, 4, GR, 128), BF),
            pltpu.VMEM((2, 4, 4, GR, 128), BF),
            pltpu.VMEM((3, 2, 4, GR, 128), BF),
            pltpu.VMEM((2, TH, C), BF),
            pltpu.VMEM((2, TW, C), BF),
            pltpu.VMEM((8, TH, C), BF),
            dma((15,)), dma((15,)), dma((15,)), dma((15,)), dma((15,)), dma((15,)),
            dma((8,)), dma((8,)), dma((4,)), dma((4,)), dma((3,)), dma((4,)),
        ],
        compiler_params=pltpu.CompilerParams(vmem_limit_bytes=60 << 20, collective_id=1, has_side_effects=True),
        name="middle",
    )(slots, meta, wts, g2, pre, feat, g1, inp)


ORDER = ("xy", "yx", "xy")


def tail_kernel(
    own, p_down, p_right, p_diag, kcol, row0, in_pad, w_ref, half, out, sums,
    r_down, r_right, r_diag, r_k, r_row0, r_s0, fg_pad, x3i, x3f, wt, parts, r0, a1, ra, a2, rb, a3, rz,
    rh, a3h, rzh, total, tsend, trecv, hsend, hrecv, csend, crecv, dsend, drecv, esend, erecv, zsend, zrecv,
):
    ty, tx = position()
    peer, there = around(ty, tx)
    x, c, y, z, other, px, py, pz = axes(ty, tx)
    greet([peer[p] for p in AROUND] + [other] + px + py + pz)
    tile = [
        remote(p_down, r_down, tsend.at[8], trecv.at[8], peer[(1, 0)]),
        remote(p_right, r_right, tsend.at[9], trecv.at[9], peer[(0, 1)]),
        remote(p_diag, r_diag, tsend.at[10], trecv.at[10], peer[(1, 1)]),
        remote(row0, r_row0, tsend.at[11], trecv.at[11], peer[(-1, 0)]),
        remote(p_right.at[0], r_s0, tsend.at[12], trecv.at[12], peer[(-1, 1)]),
    ]
    for i, (a, b) in enumerate(AROUND):
        src = kcol.at[0 if b < 0 else 1 if b > 0 else 2]
        tile.append(remote(src, r_k.at[7 - i], tsend.at[i], trecv.at[7 - i], peer[(a, b)]))
    go(tile)
    hy = go([remote(half.at[:, lax.rem(y + k, 4)], rh.at[k - 1], hsend.at[k - 1], hrecv.at[k - 1], py[k - 1]) for k in (1, 2, 3)])
    spread(x3i, in_pad)
    fg_pad[FROWS - 16 :, :] = jnp.zeros((16, C), BF)
    flip_weights(wt, w_ref)
    settle(hy)
    a3h[...] = summed(half[:, y], rh).astype(BF)
    hz = go([remote(a3h, rzh.at[k - 1], hsend.at[2 + k], hrecv.at[2 + k], pz[k - 1]) for k in (1, 2, 3)])
    settle(tile)

    up, left, right, below = there[(-1, 0)], there[(0, -1)], there[(0, 1)], there[(1, 0)]
    upleft, belowleft = there[(-1, -1)], there[(1, -1)]
    ks = {p: jnp.where(there[p], r_k[i].astype(F32), 0.0) for i, p in enumerate(AROUND)}
    own_k = kcol[2].astype(F32)
    at = lax.broadcasted_iota(jnp.int32, (16, C), 0)

    def low(v):
        s = jnp.zeros((1, C), F32)
        if 0 <= v:
            s += ks[(0, -1)][v : v + 1]
        if v <= 14:
            s += ks[(-1, -1)][16 + v : 17 + v]
        if v == 16:
            s += ks[(1, -1)][0:1]
        return s if v < 16 else jnp.where(below, s, 0.0)

    def high(v):
        s = jnp.zeros((1, C), F32)
        if 0 <= v:
            s += own_k[v : v + 1] + ks[(0, 1)][v : v + 1]
        if v <= 14:
            s += ks[(-1, 0)][16 + v : 17 + v] + ks[(-1, 1)][16 + v : 17 + v]
        if v == 16:
            s += ks[(1, 0)][0:1] + ks[(1, 1)][0:1]
        s = jnp.where(right, s, 0.0)
        return s if v < 16 else jnp.where(below, s, 0.0)

    for v in range(-2, 17):
        gap = jnp.zeros((16, C), F32)
        if v >= -1:
            gap = jnp.where(at == 0, high(v), gap)
        if v <= 15:
            gap = jnp.where(at == 15, low(v + 1), gap)
        fg_pad[pl.ds(16 + (v + 1) * PW + TW, 16), :] = gap.astype(BF)
    for v in range(-1, 17):
        row = own[v] if v >= 0 else jnp.zeros((TW, C), F32)
        side = jnp.zeros((16, C), F32)
        if v <= 14:
            row = row + jnp.where(up, r_down[v + 1].astype(F32), 0.0)
            side += jnp.where(upleft, r_diag[v + 1].astype(F32), 0.0)
        if v >= 0:
            side += jnp.where(left, r_right[v].astype(F32), 0.0)
        if v == 16:
            row = row + r_row0[...].astype(F32)
            side += jnp.where(belowleft, r_s0[...].astype(F32), 0.0)
        first, rest = row[0:16] + side, row[16:]
        if v == 16:
            first, rest = jnp.where(below, first, 0.0), jnp.where(below, rest, 0.0)
        base = 16 + (v + 1) * PW
        fg_pad[pl.ds(base, 16), :] = first.astype(BF)
        fg_pad[pl.ds(base + 16, TW - 16), :] = rest.astype(BF)

    inside = lax.broadcasted_iota(jnp.int32, (TH, PW, C), 1).reshape(FM, C) < TW
    gt = jnp.where(inside, fg_pad[pl.ds(16 + PW, FM), :].astype(F32), 0.0).astype(BF).T

    def term(q):
        emit_groups(jnp.dot(gt, x3i[pl.ds(16 + q * PW, FM), :], preferred_element_type=F32), parts, q)
        return go([remote(parts.at[q, :, 1 - c], r0.at[q], csend.at[q], crecv.at[q], other)])

    def first_axis(q, swap):
        settle(swap)
        a1[q] = (parts[q, :, c].astype(F32) + r0[q].astype(F32)).astype(BF)
        copies = []
        for k in (1, 2, 3):
            if ORDER[q] == "xy":
                src, to = a1.at[q, lax.rem(x + k, 4)], px[k - 1]
            else:
                src, to = a1.at[q, :, lax.rem(y + k, 4)], py[k - 1]
            copies.append(remote(src, ra.at[q, k - 1], dsend.at[q * 3 + k - 1], drecv.at[q * 3 + k - 1], to))
        return go(copies)

    def second_axis(q, copies):
        mine = a1[q, x] if ORDER[q] == "xy" else a1[q, :, y]
        settle(copies)
        a2[q] = summed(mine, ra[q]).astype(BF)
        copies = []
        for k in (1, 2, 3):
            n, to = (lax.rem(y + k, 4), py[k - 1]) if ORDER[q] == "xy" else (lax.rem(x + k, 4), px[k - 1])
            copies.append(remote(a2.at[q, n], rb.at[q, k - 1], esend.at[q * 3 + k - 1], erecv.at[q * 3 + k - 1], to))
        return go(copies)

    def third_axis(q, copies):
        mine = a2[q, y] if ORDER[q] == "xy" else a2[q, x]
        settle(copies)
        a3[q] = summed(mine, rb[q]).astype(BF)
        return go([remote(a3.at[q], rz.at[q, k - 1], zsend.at[q * 3 + k - 1], zrecv.at[q * 3 + k - 1], pz[k - 1]) for k in (1, 2, 3)])

    def conv(n):
        rows = FM // 2
        res = conv_flipped(x3f, wt, 16 + PW + n * rows, rows, PW).astype(BF).reshape(TH // 2, PW, C)
        out[n * TH // 2 : (n + 1) * TH // 2] = res[:, 0:TW, :]

    s0 = term(0)
    s1 = term(1)
    f0 = first_axis(0, s0)
    s2 = term(2)
    f1 = first_axis(1, s1)
    spread(x3f, fg_pad)
    conv(0)
    f2 = first_axis(2, s2)
    e0 = second_axis(0, f0)
    conv(1)
    e1 = second_axis(1, f1)
    z0 = third_axis(0, e0)
    e2 = second_axis(2, f2)
    z1 = third_axis(1, e1)
    z2 = third_axis(2, e2)
    settle(hz)
    total[0:2] = summed(a3h[...], rzh)
    for q, copies in enumerate((z0, z1, z2)):
        settle(copies)
        total[2, q * 48 : (q + 1) * 48] = summed(a3[q], rz[q])
    for t in range(3):
        for bit in range(2):
            sums[t, bit * 18 : (bit + 1) * 18, :] = total[t, pl.ds(2 * z + bit, 18, stride=8), :]


def tail(own, p_down, p_right, p_diag, kcol, row0, in_pad, w, half):
    vm = whole(None)
    dma = pltpu.SemaphoreType.DMA
    return pl.pallas_call(
        tail_kernel,
        in_specs=[vm] * 9,
        out_specs=[vm] * 2,
        out_shape=[jax.ShapeDtypeStruct((TH, TW, C), BF), jax.ShapeDtypeStruct((3, 36, 128), F32)],
        scratch_shapes=[
            pltpu.VMEM((TH, TW, C), BF),
            pltpu.VMEM((TH + 1, 16, C), BF),
            pltpu.VMEM((TH, 16, C), BF),
            pltpu.VMEM((8, 32, C), BF),
            pltpu.VMEM((TW, C), BF),
            pltpu.VMEM((16, C), BF),
            pltpu.VMEM((FROWS, C), BF),
            pltpu.VMEM((FROWS, 3 * C), BF),
            pltpu.VMEM((FROWS, 3 * C), BF),
            pltpu.VMEM((3, 3 * C, C), BF),
            pltpu.VMEM((3, 4, 2, 4, 48, 128), BF),
            pltpu.VMEM((3, 4, 4, 48, 128), BF),
            pltpu.VMEM((3, 4, 4, 48, 128), BF),
            pltpu.VMEM((3, 3, 4, 48, 128), BF),
            pltpu.VMEM((3, 4, 48, 128), BF),
            pltpu.VMEM((3, 3, 48, 128), BF),
            pltpu.VMEM((3, 48, 128), BF),
            pltpu.VMEM((3, 3, 48, 128), BF),
            pltpu.VMEM((3, 2, GR, 128), BF),
            pltpu.VMEM((2, GR, 128), BF),
            pltpu.VMEM((3, 2, GR, 128), BF),
            pltpu.VMEM((3, GR, 128), F32),
            dma((13,)), dma((13,)), dma((6,)), dma((6,)), dma((3,)), dma((3,)),
            dma((9,)), dma((9,)), dma((9,)), dma((9,)), dma((9,)), dma((9,)),
        ],
        compiler_params=pltpu.CompilerParams(vmem_limit_bytes=60 << 20, collective_id=2, has_side_effects=True),
        name="tail",
    )(own, p_down, p_right, p_diag, kcol, row0, in_pad, w, half)


def local(roi_feat, pre_one, grad_two, w_one, w_two, roi_rows, roi_cols, target_col, off_row, off_col, fpn_input, fpn_grad, w_fpn):
    slots, g1, meta, wts = front(target_col[:, 0], off_row, off_col, pre_one, grad_two, w_two, w_one, roi_rows, roi_cols)
    slots_in, meta_in, wts_in, half, in_pad = middle(slots, meta, wts, grad_two, pre_one, roi_feat, g1, fpn_input)
    own, p_down, p_right, p_diag, kcol, row0 = place(meta_in, slots_in, wts_in.reshape(512, 128), fpn_grad)
    grad_in, sums = tail(own, p_down, p_right, p_diag, kcol, row0, in_pad, w_fpn, half)
    return grad_in, sums[0].reshape(-1), sums[1].reshape(-1), sums[2].reshape(-1)


def solution(mesh):
    both = ("ty", "tx")
    placed = (
        P(both, None, None, None),
        P(both, None, None, None),
        P(both, None, None, None),
        P(),
        P(),
        P(both, None, None),
        P(both, None, None),
        P(both, None),
        P(both),
        P(both),
        P("ty", "tx", None),
        P("ty", "tx", None),
        P(),
    )
    return jax.shard_map(
        local,
        mesh=mesh,
        in_specs=placed,
        out_specs=(P("ty", "tx", None), P(both), P(both), P(both)),
        check_vma=False,
    )
```

time: 169 us -> 130 us (0.77)
  Pallas kernels: 157 us -> 127 us
  starting transfers between devices: 8.23 us -> 0 us
    pallas_call x6 -> x3, Pallas kernels: 132 us -> 107 us  [the longest x1 54.4 us: middle(): pl.pallas_call(middle_kernel, in_specs=[hbm, vm, vm, hbm, hbm, hbm, hbm,...]
    all_to_all x1 -> x0, starting transfers between devices: 8.23 us -> none  [local(): lax.all_to_all(win.reshape(16, 512, C), 'tx', split_axis=0, concat_axis=0...]
    pallas_call x1, Pallas kernels: 24.5 us -> 20.5 us  [front(): pl.pallas_call(front_kernel, grid_spec=pltpu.PrefetchScalarGridSpec(num_s...]
  transfers between devices with their start and end apart: 1 -> 0, of which waited for: 0 -> 0; matrix products, arithmetic and copies ran while one was open for 1% -> 0% of each run, Pallas kernels for 41% -> 0%
where the time goes in v2:
time: 130 us; the launch traced here: 131 us
  Pallas kernels  127 us (98%)
  local copies, waits for them, and re-layouts  3.27 us (3%)
    pallas_call x1, Pallas kernels, middle(): pl.pallas_call(middle_kernel, in_specs=[hbm, vm, vm, hbm, hbm, hbm, hbm,...  54.4 us
    pallas_call x1, Pallas kernels, tail(): pl.pallas_call(tail_kernel, in_specs=[vm] * 9, out_specs=[vm] * 2, out_sh...  41.7 us
    pallas_call x1, Pallas kernels, front(): pl.pallas_call(front_kernel, grid_spec=pltpu.PrefetchScalarGridSpec(num_s...  20.5 us
    pallas_call x1, Pallas kernels, place(): pl.pallas_call(place_kernel, in_specs=[whole(None, pltpu.SMEM)] + [whole(...  10.5 us

profile of v2, /device:TPU:0, one launch (start us, length us, event | category | flops | bytes accessed | tf_op | source)
XLA Modules:
  0.0 131.0 jit_solution(2916832576805598260)
XLA Ops:
  0.6 20.5 %front.1 = (bf16[16,2,200,256]{3,2,1,0:T(8,128)(2,1)}, bf16[12,240,256]{2,1,0:T(8,128)(2,1)}, s32[16,8,128]{2,1,0:T(8,128)}, bf16[16,2,16,128]{3,2,1,0:T(8,128)(2,1)}) custom-call(s32[12]{0:T(128)} %bitcast.9, s32[12]{0:T(128)} %orow.1, s32[12]{0:T(128)} %ocol.1, bf16[12,14,14,256]{3,2,1,0:T(8,128)(2,1)} %pre.1, bf16[12,14,14,256]{3,2,1,0:T(8,128)(2,1)} %g2.1, ...), custom_call_target="tpu_custom_call" | custom-call | flops 8000000000 | bytes 12582912 | tf_op jit(solution)/shard_map/front/pallas_call | solution.py:99
  21.1 54.4 %middle.1 = (bf16[16,2,200,256]{3,2,1,0:T(8,128)(2,1)}, s32[16,8,128]{2,1,0:T(8,128)}, bf16[16,2,16,128]{3,2,1,0:T(8,128)(2,1)}, bf16[2,4,144,128]{3,2,1,0:T(8,128)(2,1)}, bf16[1472,256]{1,0:T(8,128)(2,1)}) custom-call(bf16[16,2,200,256]{3,2,1,0:T(8,128)(2,1)} %get-tuple-element.21.slots, s32[16,8,128]{2,1,0:T(8,128)} %get-tuple-element.22.meta, ...), custom_call_target="tpu_custom_call" | custom-call | tf_op jit(solution)/shard_map/middle/pallas_call | solution.py:353
  75.5 10.5 %place.1 = (f32[17,64,256]{2,1,0:T(8,128)}, bf16[16,64,256]{2,1,0:T(8,128)(2,1)}, bf16[17,16,256]{2,1,0:T(8,128)(2,1)}, bf16[16,16,256]{2,1,0:T(8,128)(2,1)}, bf...) custom-call(s32[16,8,128]{2,1,0:T(8,128)} %get-tuple-element.25.meta, ...), custom_call_target="tpu_custom_call" | custom-call | tf_op jit(solution)/shard_map/place/pallas_call | solution.py:180
  86.0 41.7 %tail.1 = (bf16[16,64,256]{2,1,0:T(8,128)(2,1)}, f32[3,36,128]{2,1,0:T(8,128)}) custom-call(f32[17,64,256]{2,1,0:T(8,128)} %get-tuple-element.28.own, bf16[16,64,256]{2,1,0:T(8,128)(2,1)} %get-tuple-element.29.p_down, bf16[17,16,256]{2,1,0:T(8,128)(2,1)} %get-tuple-element.30.p_right, bf16[16,16,256]{2,1,0:T(8,128)(2,1)} %get-tuple-element.31.p_diag, ...), custom_call_target="tpu_custom_call" | custom-call | tf_op jit(solution)/shard_map/tail/pallas_call | solution.py:541
  127.7 1.4 %slice_bitcast_fusion = (f32[4608]{0:T(1024)}, f32[4608]{0:T(1024)}, f32[4608]{0:T(1024)}) fusion(f32[3,36,128]{2,1,0:T(8,128)} %get-tuple-element.37), kind=kLoop, calls=%fused_computation | loop fusion | bytes 110592 | tf_op jit(solution)/shard_map/reshape;squeeze | solution.py:582
  129.1 1.9 %copy.18 = bf16[16,64,256]{2,1,0:T(8,128)(2,1)} copy(bf16[16,64,256]{2,1,0:T(8,128)(2,1)} %get-tuple-element.45) | data formatting | bytes 1048576

commit v3 on v2

v3 whole, which is shorter than its diff:
```python
import jax
import jax.numpy as jnp
from jax import lax
from jax.experimental import pallas as pl
from jax.experimental.pallas import tpu as pltpu
from jax.sharding import PartitionSpec as P

F32, BF = jnp.float32, jnp.bfloat16
MESH = pl.DeviceIdType.MESH
C = 256
NB, RB = 4, 240
SR = 200
M = NB * RB
TH, TW, PW = 16, 64, 80
FM = TH * PW
FROWS = 16 + 18 * PW + 16
GR = 144
NT = (((1,), (1,)), ((), ()))
VM = pltpu.CompilerParams(vmem_limit_bytes=60 << 20)


def whole(shape, space=pltpu.VMEM):
    return pl.BlockSpec(memory_space=space)


def fixed(shape):
    zeros = (0,) * len(shape)
    return pl.BlockSpec(shape, lambda *_: zeros, pipeline_mode=pl.Buffered(1))


def load_padded(dst, src, fn=None, first=0):
    for r in range(NB):
        for y in range(14):
            v = src[first + r, y]
            dst[pl.ds(16 + r * RB + y * 16, 14), :] = v if fn is None else fn(v)


def spread(x3, v):
    n = v.shape[0]
    x3[:, 256:512] = v[...]
    x3[pl.ds(1, n - 1), 0:256] = v[pl.ds(0, n - 1), :]
    x3[pl.ds(0, n - 1), 512:768] = v[pl.ds(1, n - 1), :]


def line_up(wt, w):
    for dy in range(3):
        for kk in range(3):
            wt[dy, :, kk * C : (kk + 1) * C] = w[dy, 2 - kk]


def conv_flipped(x3, wt, base, rows, pitch):
    acc = None
    for dy in range(3):
        t = lax.dot_general(x3[pl.ds(base + (1 - dy) * pitch, rows), :], wt[dy], NT, preferred_element_type=F32)
        acc = t if acc is None else acc + t
    return acc


def front_kernel(tgt, orow, ocol, pre_ref, g2_ref, w2_ref, w1_ref, rows_ref, cols_ref, slot_ref, g1_ref, meta_ref, wts_ref, vb, x3, vp, wt2, wt1):
    step = pl.program_id(0)

    @pl.when(step == 0)
    def _():
        vb[...] = jnp.zeros_like(vb)
        vp[...] = jnp.zeros_like(vp)
        x3[0:16] = jnp.zeros((16, 3 * C), BF)
        x3[M + 16 :] = jnp.zeros((16, 3 * C), BF)
        meta_ref[...] = jnp.zeros_like(meta_ref)
        wts_ref[...] = jnp.zeros_like(wts_ref)
        slot_ref[...] = jnp.zeros_like(slot_ref)
        line_up(wt2, w2_ref)
        line_up(wt1, w1_ref)

    load_padded(vb, g2_ref)
    load_padded(vp, pre_ref)
    spread(x3, vb)
    b2 = conv_flipped(x3, wt2, 16, M, 16)
    g1 = jnp.where(vp[pl.ds(16, M), :] > 0, b2, 0.0).astype(BF)
    g1_ref[...] = g1.reshape(NB, RB, C)
    vb[pl.ds(16, M), :] = g1
    spread(x3, vb)
    rg = conv_flipped(x3, wt1, 16, M, 16).astype(BF)
    lanes = lax.broadcasted_iota(jnp.int32, (8, 128), 1)
    for r in range(NB):
        at = step * NB + r
        t = tgt[at]
        k = lax.fori_loop(0, at, lambda q, s: s + jnp.where(tgt[q] == t, 1, 0), 0)
        for i in range(14):
            slot_ref[t, k, pl.ds(i * 14, 14), :] = rg[r * RB + i * 16 : r * RB + i * 16 + 14]
        old = meta_ref[t]
        new = jnp.where(lanes == 4 * k, 1, old)
        new = jnp.where(lanes == 4 * k + 1, orow[at], new)
        meta_ref[t] = jnp.where(lanes == 4 * k + 2, ocol[at], new)
        wts_ref[t, k, :, 0:14] = rows_ref[r]
        wts_ref[t, k, :, 16:30] = cols_ref[r]


def front(tgt, orow, ocol, pre, g2, w2, w1, rows, cols):
    blk = pl.BlockSpec((NB, 14, 14, C), lambda i, *_: (i, 0, 0, 0))
    rspec = pl.BlockSpec((NB, 16, 14), lambda i, *_: (i, 0, 0))
    return pl.pallas_call(
        front_kernel,
        grid_spec=pltpu.PrefetchScalarGridSpec(
            num_scalar_prefetch=3,
            grid=(3,),
            in_specs=[blk, blk, fixed((3, 3, C, C)), fixed((3, 3, C, C)), rspec, rspec],
            out_specs=[
                fixed((16, 2, SR, C)),
                pl.BlockSpec((NB, RB, C), lambda i, *_: (i, 0, 0)),
                fixed((16, 8, 128)),
                fixed((16, 2, 16, 128)),
            ],
            scratch_shapes=[
                pltpu.VMEM((M + 32, C), BF),
                pltpu.VMEM((M + 32, 3 * C), BF),
                pltpu.VMEM((M + 32, C), BF),
                pltpu.VMEM((3, C, 3 * C), BF),
                pltpu.VMEM((3, C, 3 * C), BF),
            ],
        ),
        out_shape=[
            jax.ShapeDtypeStruct((16, 2, SR, C), BF),
            jax.ShapeDtypeStruct((12, RB, C), BF),
            jax.ShapeDtypeStruct((16, 8, 128), jnp.int32),
            jax.ShapeDtypeStruct((16, 2, 16, 128), BF),
        ],
        compiler_params=VM,
        cost_estimate=pl.CostEstimate(flops=8 * 10**9, bytes_accessed=12 << 20, transcendentals=0),
        name="front",
    )(tgt, orow, ocol, pre, g2, w2, w1, rows, cols)


def emit_groups(value, out, lead):
    for g in range(32):
        for j in range(value.shape[1] // 256):
            lo = value[g * 8 : (g + 1) * 8, j * 256 : j * 256 + 128]
            hi = value[g * 8 : (g + 1) * 8, j * 256 + 128 : (j + 1) * 256]
            both = jnp.concatenate([lo, hi], axis=0).astype(BF)
            out[lead, g // 8, g // 4 % 2, g % 4, j * 16 : (j + 1) * 16, :] = both


def position():
    return lax.axis_index("ty"), lax.axis_index("tx")


def greet(peers):
    barrier = pltpu.get_barrier_semaphore()
    for peer in peers:
        pl.semaphore_signal(barrier, inc=1, device_id=peer, device_id_type=MESH)
    pl.semaphore_wait(barrier, len(peers))


def remote(src, dst, send, recv, peer):
    return pltpu.make_async_remote_copy(src, dst, send, recv, device_id=peer, device_id_type=MESH)


def go(copies):
    for copy in copies:
        copy.start()
    return copies


def settle(copies):
    for copy in copies:
        copy.wait()


def summed(mine, got):
    return mine.astype(F32) + got[0].astype(F32) + got[1].astype(F32) + got[2].astype(F32)


AROUND = [(-1, -1), (-1, 0), (-1, 1), (0, -1), (0, 1), (1, -1), (1, 0), (1, 1)]
ROW = [(0, 1), (1, 0), (0, 3), (3, 0), (1, 1), (3, 3), (1, 3), (3, 1), (0, 2), (2, 0), (1, 2), (2, 1), (3, 2), (2, 3), (2, 2)]


def around(ty, tx):
    peer = {(a, b): (lax.rem(ty + a + 8, 8), lax.rem(tx + b + 16, 16)) for a, b in AROUND}
    there = {
        (a, b): (ty + a >= 0) & (ty + a < 8) & (tx + b >= 0) & (tx + b < 16) for a, b in AROUND
    }
    return peer, there


def axes(ty, tx):
    x, c, y, z = ty // 2, ty % 2, tx // 4, tx % 4
    other = (x * 2 + 1 - c, tx)
    px = [(lax.rem(x + k, 4) * 2 + c, tx) for k in (1, 2, 3)]
    py = [(ty, lax.rem(y + k, 4) * 4 + z) for k in (1, 2, 3)]
    pz = [(ty, y * 4 + lax.rem(z + k, 4)) for k in (1, 2, 3)]
    return x, c, y, z, other, px, py, pz


def pad_input(block, pad, rows_in, cols_in, there):
    zero = jnp.zeros((16, C), F32)
    at = lax.broadcasted_iota(jnp.int32, (16, C), 0)

    def column(a, b):
        return jnp.where(there[(a, b)], cols_in[AROUND.index((a, b))].astype(F32), 0.0)

    low = [column(-1, -1), column(0, -1), column(1, -1)]
    high = [column(-1, 1), column(0, 1), column(1, 1)]

    def edge(parts, y):
        v, r = (parts[0], 15) if y < 0 else (parts[2], 0) if y > 15 else (parts[1], y)
        return v[r : r + 1, :]

    for y in range(-2, 17):
        gap = zero
        if y >= -1:
            gap = jnp.where(at == 0, edge(high, y), gap)
        if y <= 15:
            gap = jnp.where(at == 15, edge(low, y + 1), gap)
        pad[pl.ds(16 + (y + 1) * PW + TW, 16), :] = gap.astype(BF)
    pad[FROWS - 16 :, :] = jnp.zeros((16, C), BF)
    for k, a in ((0, -1), (1, 1)):
        row = jnp.where(there[(a, 0)], rows_in[k].astype(F32), 0.0).astype(BF)
        pad[pl.ds(16 + (0 if a < 0 else 17) * PW, TW), :] = row
    for y in range(TH):
        pad[pl.ds(16 + (y + 1) * PW, TW), :] = block[y]


ORDER = ("xy", "yx", "xy")
ARRIVALS = ((15, 16), (0, 4), (4, 8), (8, 12), (12, 14), (14, 15))
SCRATCH = {}


def rest_kernel(slots, meta, wts, g2, pre, feat, g1, inp, grad, w, out, sums, *scratch):
    r = dict(zip(SCRATCH, scratch))
    ty, tx = position()
    peer, there = around(ty, tx)
    x, c, y, z, other, px, py, pz = axes(ty, tx)
    row = [(ty, lax.rem(y + dy, 4) * 4 + lax.rem(z + dz, 4)) for dy, dz in ROW]
    pairs = ((inp, "inp"), (pre, "pre"), (g2, "g2"), (feat, "feat"), (g1, "g1"), (grad, "grad"), (w, "w"))
    loads = go([pltpu.make_async_copy(src, r[name], r["fetch"].at[i]) for i, (src, name) in enumerate(pairs)])
    greet([peer[p] for p in AROUND] + row + [other] + px)
    slots_in, meta_in, wts_in = r["slots_in"], r["meta_in"], r["wts_in"]
    tile_in, cols_out = r["inp"], r["cols_out"]
    to = [q[1] for q in row]
    letters = go([remote(meta.at[q], meta_in.at[i], r["msend"].at[i], r["mrecv"].at[i], row[i]) for i, q in enumerate(to)])
    letters += go([remote(wts.at[q], wts_in.at[i], r["wsend"].at[i], r["wrecv"].at[i], row[i]) for i, q in enumerate(to)])
    loads[0].wait()
    cols_out[0] = tile_in[:, 0, :]
    cols_out[1] = tile_in[:, TW - 1, :]
    halo = []
    for i, (a, b) in enumerate(AROUND):
        if b == 0:
            src, dst = tile_in.at[0 if a < 0 else TH - 1], r["rows_in"].at[1 if a < 0 else 0]
        else:
            src, dst = cols_out.at[0 if b < 0 else 1], r["cols_in"].at[7 - i]
        halo.append(remote(src, dst, r["hsend"].at[i], r["hrecv"].at[7 - i], peer[(a, b)]))
    go(halo)
    sent = go([remote(slots.at[q], slots_in.at[i], r["asend"].at[i], r["arecv"].at[i], row[i]) for i, q in enumerate(to)])
    kept = go([
        pltpu.make_async_copy(slots.at[tx], slots_in.at[15], r["keep"].at[0]),
        pltpu.make_async_copy(meta.at[tx], meta_in.at[15], r["keep"].at[1]),
        pltpu.make_async_copy(wts.at[tx], wts_in.at[15], r["keep"].at[2]),
    ])

    vb, vx, x3, acc2, acc1, hparts = r["vb"], r["vx"], r["x3"], r["acc2"], r["acc1"], r["hparts"]
    for buf in (vb, vx, acc2, acc1):
        buf[...] = jnp.zeros_like(buf)
    x3[0:16] = jnp.zeros((16, 3 * C), BF)
    x3[M + 16 :] = jnp.zeros((16, 3 * C), BF)
    settle(loads[1:])

    def step(n, carry):
        load_padded(vx, r["pre"], lambda v: jnp.maximum(v, 0), n * NB)
        spread(x3, vx)
        load_padded(vb, r["g2"], None, n * NB)
        gt = vb[pl.ds(16, M), :].T
        for dy in range(3):
            acc2[:, dy * 768 : (dy + 1) * 768] += jnp.dot(gt, x3[pl.ds(dy * 16, M), :], preferred_element_type=F32)
        load_padded(vx, r["feat"], None, n * NB)
        spread(x3, vx)
        gt = r["g1"][pl.ds(n * NB, NB)].reshape(M, C).T
        for dy in range(3):
            acc1[:, dy * 768 : (dy + 1) * 768] += jnp.dot(gt, x3[pl.ds(dy * 16, M), :], preferred_element_type=F32)
        return carry

    lax.fori_loop(0, 3, step, 0)
    emit_groups(acc1, hparts, 0)
    emit_groups(acc2, hparts, 1)
    swap = go([remote(hparts.at[:, :, 1 - c], r["hr0"], r["ssend"].at[0], r["srecv"].at[0], other)])

    settle(letters)
    settle(kept)
    listed = pltpu.make_async_copy(meta_in, r["smeta"], r["listed"])
    listed.start()
    smeta, canvas, wp, rl, cl = r["smeta"], r["canvas"], r["wp"], r["rl"], r["cl"]
    canvas[...] = jnp.zeros_like(canvas)
    wp[...] = jnp.zeros_like(wp)
    lane = lax.broadcasted_iota(jnp.int32, (128, 256), 1)
    at = lax.broadcasted_iota(jnp.int32, (128, 256), 0)
    bin_row = lane // 14
    bin_col = lane - bin_row * 14
    used = lane < 196
    both_w = wts_in[...].reshape(512, 128)
    rl[...] = jnp.dot(both_w, (used & (bin_row == at)).astype(BF), preferred_element_type=F32).reshape(32, 16, 256)
    cl[...] = jnp.dot(both_w, (used & (bin_col + 16 == at)).astype(BF), preferred_element_type=F32).reshape(32, 16, 256)
    for h in range(2):
        canvas[h, 0:TH, 0:TW, :] = r["grad"][:, :, h * 128 : (h + 1) * 128].astype(F32)
    settle(swap)
    ha1 = r["ha1"]
    for xx in range(4):
        ha1[:, xx] = (hparts[:, xx, c].astype(F32) + r["hr0"][:, xx].astype(F32)).astype(BF)
    cross = go([remote(ha1.at[:, lax.rem(x + k, 4)], r["hr1"].at[k - 1], r["ssend"].at[k], r["srecv"].at[k], px[k - 1]) for k in (1, 2, 3)])
    settle(halo)
    in_pad, x3i, x3f, wt, fg_pad = r["in_pad"], r["x3i"], r["x3f"], r["wt"], r["fg_pad"]
    pad_input(tile_in, in_pad, r["rows_in"], r["cols_in"], there)
    spread(x3i, in_pad)
    line_up(wt, r["w"])
    fg_pad[FROWS - 16 :, :] = jnp.zeros((16, C), BF)
    listed.wait()

    def put(s, carry):
        i, k = s // 2, s % 2
        top = 15 - smeta[i, 0, 4 * k + 1]
        side = TW - smeta[i, 0, 4 * k + 2]
        both = (rl[s][:, None, :] * cl[s][None, :, :]).reshape(256, 256).astype(BF)
        win = jnp.dot(both[:, 0:196], slots_in[i, k, 0:196, :], preferred_element_type=F32)
        for h in range(2):
            wp[h, 15:31, TW : TW + 16, :] = win[:, h * 128 : (h + 1) * 128].reshape(16, 16, 128)
        for v in range(31):
            for h in range(2):
                canvas[h, v] += wp[h, top + v, pl.ds(side, PW), :]
        return carry

    for n, (first, last) in enumerate(ARRIVALS):
        if n:
            for i in range(first, last):
                sent[i].wait_recv()
        lax.fori_loop(2 * first, 2 * last, put, 0)
        if n == 1:
            settle(cross)
            half = r["half"]
            half[...] = summed(ha1[:, x], r["hr1"]).astype(BF)

    p_down, p_right, p_diag, kcol, row0 = r["p_down"], r["p_right"], r["p_diag"], r["kcol"], r["row0"]
    for h in range(2):
        part = slice(h * 128, (h + 1) * 128)
        p_down[:, :, part] = canvas[h, TH - 1 : 31, 0:TW, :].astype(BF)
        p_right[:, :, part] = canvas[h, 0 : TH + 1, TW:PW, :].astype(BF)
        p_diag[:, :, part] = canvas[h, TH - 1 : 31, TW:PW, :].astype(BF)
        for n, col in enumerate((0, TW - 1, TW)):
            kcol[n, :, part] = canvas[h, :, col, :].astype(BF)
        row0[:, part] = canvas[h, 0, 0:TW, :].astype(BF)
    tsend, trecv = r["tsend"], r["trecv"]
    r_down, r_right, r_diag, r_k, r_row0, r_s0 = (r[q] for q in ("r_down", "r_right", "r_diag", "r_k", "r_row0", "r_s0"))
    tile = [
        remote(p_down, r_down, tsend.at[8], trecv.at[8], peer[(1, 0)]),
        remote(p_right, r_right, tsend.at[9], trecv.at[9], peer[(0, 1)]),
        remote(p_diag, r_diag, tsend.at[10], trecv.at[10], peer[(1, 1)]),
        remote(row0, r_row0, tsend.at[11], trecv.at[11], peer[(-1, 0)]),
        remote(p_right.at[0], r_s0, tsend.at[12], trecv.at[12], peer[(-1, 1)]),
    ]
    for i, (a, b) in enumerate(AROUND):
        src = kcol.at[0 if b < 0 else 1 if b > 0 else 2]
        tile.append(remote(src, r_k.at[7 - i], tsend.at[i], trecv.at[7 - i], peer[(a, b)]))
    go(tile)
    hy = go([remote(half.at[:, lax.rem(y + k, 4)], r["rh"].at[k - 1], r["ysend"].at[k - 1], r["yrecv"].at[k - 1], py[k - 1]) for k in (1, 2, 3)])
    for copy in sent:
        copy.wait_send()
    settle(tile)
    parts, r0, a1, ra, a2, rb, a3, rz, rh, a3h, rzh, total, csend, crecv, dsend, drecv, esend, erecv, zsend, zrecv = (
        r[q] for q in (
            "parts", "r0", "a1", "ra", "a2", "rb", "a3", "rz", "rh", "a3h", "rzh", "total", "csend", "crecv", "dsend", "drecv", "esend", "erecv", "zsend", "zrecv",
        )
    )
    up, left, right, below = there[(-1, 0)], there[(0, -1)], there[(0, 1)], there[(1, 0)]
    upleft, belowleft = there[(-1, -1)], there[(1, -1)]
    ks = {p: jnp.where(there[p], r_k[i].astype(F32), 0.0) for i, p in enumerate(AROUND)}
    own_k = kcol[2].astype(F32)
    at = lax.broadcasted_iota(jnp.int32, (16, C), 0)

    def low(v):
        s = jnp.zeros((1, C), F32)
        if 0 <= v:
            s += ks[(0, -1)][v : v + 1]
        if v <= 14:
            s += ks[(-1, -1)][16 + v : 17 + v]
        if v == 16:
            s += ks[(1, -1)][0:1]
        return s if v < 16 else jnp.where(below, s, 0.0)

    def high(v):
        s = jnp.zeros((1, C), F32)
        if 0 <= v:
            s += own_k[v : v + 1] + ks[(0, 1)][v : v + 1]
        if v <= 14:
            s += ks[(-1, 0)][16 + v : 17 + v] + ks[(-1, 1)][16 + v : 17 + v]
        if v == 16:
            s += ks[(1, 0)][0:1] + ks[(1, 1)][0:1]
        s = jnp.where(right, s, 0.0)
        return s if v < 16 else jnp.where(below, s, 0.0)

    for v in range(-2, 17):
        gap = jnp.zeros((16, C), F32)
        if v >= -1:
            gap = jnp.where(at == 0, high(v), gap)
        if v <= 15:
            gap = jnp.where(at == 15, low(v + 1), gap)
        fg_pad[pl.ds(16 + (v + 1) * PW + TW, 16), :] = gap.astype(BF)
    for v in range(-1, 17):
        for h in range(2):
            part = slice(h * 128, (h + 1) * 128)
            line = canvas[h, v, 0:TW, :] if v >= 0 else jnp.zeros((TW, 128), F32)
            side = jnp.zeros((16, 128), F32)
            if v <= 14:
                line = line + jnp.where(up, r_down[v + 1, :, part].astype(F32), 0.0)
                side += jnp.where(upleft, r_diag[v + 1, :, part].astype(F32), 0.0)
            if v >= 0:
                side += jnp.where(left, r_right[v, :, part].astype(F32), 0.0)
            if v == 16:
                line = line + r_row0[:, part].astype(F32)
                side += jnp.where(belowleft, r_s0[:, part].astype(F32), 0.0)
            first, others = line[0:16] + side, line[16:]
            if v == 16:
                first, others = jnp.where(below, first, 0.0), jnp.where(below, others, 0.0)
            base = 16 + (v + 1) * PW
            fg_pad[pl.ds(base, 16), part] = first.astype(BF)
            fg_pad[pl.ds(base + 16, TW - 16), part] = others.astype(BF)

    inside = lax.broadcasted_iota(jnp.int32, (TH, PW, C), 1).reshape(FM, C) < TW
    gt = jnp.where(inside, fg_pad[pl.ds(16 + PW, FM), :].astype(F32), 0.0).astype(BF).T

    def term(q):
        emit_groups(jnp.dot(gt, x3i[pl.ds(16 + q * PW, FM), :], preferred_element_type=F32), parts, q)
        return go([remote(parts.at[q, :, 1 - c], r0.at[q], csend.at[q], crecv.at[q], other)])

    def first_axis(q, swap):
        settle(swap)
        a1[q] = (parts[q, :, c].astype(F32) + r0[q].astype(F32)).astype(BF)
        copies = []
        for k in (1, 2, 3):
            if ORDER[q] == "xy":
                src, to = a1.at[q, lax.rem(x + k, 4)], px[k - 1]
            else:
                src, to = a1.at[q, :, lax.rem(y + k, 4)], py[k - 1]
            copies.append(remote(src, ra.at[q, k - 1], dsend.at[q * 3 + k - 1], drecv.at[q * 3 + k - 1], to))
        return go(copies)

    def second_axis(q, copies):
        mine = a1[q, x] if ORDER[q] == "xy" else a1[q, :, y]
        settle(copies)
        a2[q] = summed(mine, ra[q]).astype(BF)
        copies = []
        for k in (1, 2, 3):
            n, to = (lax.rem(y + k, 4), py[k - 1]) if ORDER[q] == "xy" else (lax.rem(x + k, 4), px[k - 1])
            copies.append(remote(a2.at[q, n], rb.at[q, k - 1], esend.at[q * 3 + k - 1], erecv.at[q * 3 + k - 1], to))
        return go(copies)

    def third_axis(q, copies):
        mine = a2[q, y] if ORDER[q] == "xy" else a2[q, x]
        settle(copies)
        a3[q] = summed(mine, rb[q]).astype(BF)
        return go([remote(a3.at[q], rz.at[q, k - 1], zsend.at[q * 3 + k - 1], zrecv.at[q * 3 + k - 1], pz[k - 1]) for k in (1, 2, 3)])

    def conv(n):
        rows = FM // 2
        res = conv_flipped(x3f, wt, 16 + PW + n * rows, rows, PW).astype(BF).reshape(TH // 2, PW, C)
        out[n * TH // 2 : (n + 1) * TH // 2] = res[:, 0:TW, :]

    settle(hy)
    a3h[...] = summed(half[:, y], rh).astype(BF)
    hz = go([remote(a3h, rzh.at[k - 1], r["ysend"].at[2 + k], r["yrecv"].at[2 + k], pz[k - 1]) for k in (1, 2, 3)])
    s0 = term(0)
    s1 = term(1)
    f0 = first_axis(0, s0)
    s2 = term(2)
    f1 = first_axis(1, s1)
    spread(x3f, fg_pad)
    conv(0)
    f2 = first_axis(2, s2)
    e0 = second_axis(0, f0)
    conv(1)
    e1 = second_axis(1, f1)
    z0 = third_axis(0, e0)
    e2 = second_axis(2, f2)
    z1 = third_axis(1, e1)
    z2 = third_axis(2, e2)
    settle(hz)
    total[0:2] = summed(a3h[...], rzh)
    for q, copies in enumerate((z0, z1, z2)):
        settle(copies)
        total[2, q * 48 : (q + 1) * 48] = summed(a3[q], rz[q])
    for t in range(3):
        for bit in range(2):
            sums[t, bit * 18 : (bit + 1) * 18, :] = total[t, pl.ds(2 * z + bit, 18, stride=8), :]


def rest(slots, meta, wts, g2, pre, feat, g1, inp, grad, w):
    hbm = whole(None, pltpu.HBM)
    vm = whole(None)
    dma = pltpu.SemaphoreType.DMA
    regions = (12, 14, 14, C)
    SCRATCH.clear()
    for name, shape in (
        ("inp", (TH, TW, C)), ("pre", regions), ("g2", regions), ("feat", regions), ("g1", (12, RB, C)),
        ("grad", (TH, TW, C)), ("w", (3, 3, C, C)),
        ("slots_in", (16, 2, SR, C)), ("wts_in", (16, 2, 16, 128)),
        ("vb", (M + 32, C)), ("vx", (M + 32, C)), ("x3", (M + 32, 3 * C)),
        ("hparts", (2, 4, 2, 4, GR, 128)), ("hr0", (2, 4, 4, GR, 128)), ("ha1", (2, 4, 4, GR, 128)),
        ("hr1", (3, 2, 4, GR, 128)), ("half", (2, 4, GR, 128)), ("rh", (3, 2, GR, 128)),
        ("a3h", (2, GR, 128)), ("rzh", (3, 2, GR, 128)),
        ("cols_out", (2, TH, C)), ("rows_in", (2, TW, C)), ("cols_in", (8, TH, C)),
        ("p_down", (TH, TW, C)), ("p_right", (TH + 1, 16, C)), ("p_diag", (TH, 16, C)), ("kcol", (3, 32, C)), ("row0", (TW, C)),
        ("r_down", (TH, TW, C)), ("r_right", (TH + 1, 16, C)), ("r_diag", (TH, 16, C)), ("r_k", (8, 32, C)),
        ("r_row0", (TW, C)), ("r_s0", (16, C)),
        ("in_pad", (FROWS, C)), ("fg_pad", (FROWS, C)), ("x3i", (FROWS, 3 * C)), ("x3f", (FROWS, 3 * C)), ("wt", (3, C, 3 * C)),
        ("parts", (3, 4, 2, 4, 48, 128)), ("r0", (3, 4, 4, 48, 128)), ("a1", (3, 4, 4, 48, 128)), ("ra", (3, 3, 4, 48, 128)),
        ("a2", (3, 4, 48, 128)), ("rb", (3, 3, 48, 128)), ("a3", (3, 48, 128)), ("rz", (3, 3, 48, 128)),
    ):
        SCRATCH[name] = pltpu.VMEM(shape, BF)
    for name, shape in (
        ("acc2", (C, 9 * C)), ("acc1", (C, 9 * C)), ("canvas", (2, 2 * TH, PW, 128)), ("wp", (2, 46, 144, 128)),
        ("rl", (32, 16, 256)), ("cl", (32, 16, 256)), ("total", (3, GR, 128)),
    ):
        SCRATCH[name] = pltpu.VMEM(shape, F32)
    SCRATCH["meta_in"] = pltpu.VMEM((16, 8, 128), jnp.int32)
    SCRATCH["smeta"] = pltpu.SMEM((16, 8, 128), jnp.int32)
    for name, n in (
        ("fetch", 7), ("msend", 15), ("mrecv", 15), ("wsend", 15), ("wrecv", 15), ("asend", 15), ("arecv", 15),
        ("hsend", 8), ("hrecv", 8), ("keep", 3), ("ssend", 4), ("srecv", 4), ("ysend", 6), ("yrecv", 6),
        ("tsend", 13), ("trecv", 13), ("csend", 3), ("crecv", 3), ("dsend", 9), ("drecv", 9), ("esend", 9), ("erecv", 9),
        ("zsend", 9), ("zrecv", 9),
    ):
        SCRATCH[name] = dma((n,))
    SCRATCH["listed"] = dma(())
    return pl.pallas_call(
        rest_kernel,
        in_specs=[hbm, vm, vm] + [hbm] * 7,
        out_specs=[vm] * 2,
        out_shape=[jax.ShapeDtypeStruct((TH, TW, C), BF), jax.ShapeDtypeStruct((3, 36, 128), F32)],
        scratch_shapes=list(SCRATCH.values()),
        compiler_params=pltpu.CompilerParams(vmem_limit_bytes=63 << 20, collective_id=1, has_side_effects=True),
        name="rest",
    )(slots, meta, wts, g2, pre, feat, g1, inp, grad, w)


def local(roi_feat, pre_one, grad_two, w_one, w_two, roi_rows, roi_cols, target_col, off_row, off_col, fpn_input, fpn_grad, w_fpn):
    slots, g1, meta, wts = front(target_col[:, 0], off_row, off_col, pre_one, grad_two, w_two, w_one, roi_rows, roi_cols)
    grad_in, sums = rest(slots, meta, wts, grad_two, pre_one, roi_feat, g1, fpn_input, fpn_grad, w_fpn)
    return grad_in, sums[0].reshape(-1), sums[1].reshape(-1), sums[2].reshape(-1)


def solution(mesh):
    both = ("ty", "tx")
    placed = (
        P(both, None, None, None),
        P(both, None, None, None),
        P(both, None, None, None),
        P(),
        P(),
        P(both, None, None),
        P(both, None, None),
        P(both, None),
        P(both),
        P(both),
        P("ty", "tx", None),
        P("ty", "tx", None),
        P(),
    )
    return jax.shard_map(
        local,
        mesh=mesh,
        in_specs=placed,
        out_specs=(P("ty", "tx", None), P(both), P(both), P(both)),
        check_vma=False,
    )
```

time: 130 us -> 116 us (0.89)
  Pallas kernels: 127 us -> 112 us
    pallas_call x3 -> x1, Pallas kernels: 107 us -> 91.7 us  [rest(): pl.pallas_call(rest_kernel, in_specs=[hbm, vm, vm] + [hbm] * 7, out_specs...]
where the time goes in v3:
time: 116 us
  Pallas kernels  112 us (97%)
  local copies, waits for them, and re-layouts  3.27 us (3%)
    pallas_call x1, Pallas kernels, rest(): pl.pallas_call(rest_kernel, in_specs=[hbm, vm, vm] + [hbm] * 7, out_specs...  91.7 us
    pallas_call x1, Pallas kernels, front(): pl.pallas_call(front_kernel, grid_spec=pltpu.PrefetchScalarGridSpec(num_s...  20.4 us

profile of v3, /device:TPU:0, one launch (start us, length us, event | category | flops | bytes accessed | tf_op | source)
XLA Modules:
  0.0 116.0 jit_solution(13821441586524866127)
XLA Ops:
  0.6 20.4 %front.1 = (bf16[16,2,200,256]{3,2,1,0:T(8,128)(2,1)}, bf16[12,240,256]{2,1,0:T(8,128)(2,1)}, s32[16,8,128]{2,1,0:T(8,128)}, bf16[16,2,16,128]{3,2,1,0:T(8,128)(2,1)}) custom-call(s32[12]{0:T(128)} %bitcast.7, s32[12]{0:T(128)} %orow.1, s32[12]{0:T(128)} %ocol.1, bf16[12,14,14,256]{3,2,1,0:T(8,128)(2,1)} %pre.1, bf16[12,14,14,256]{3,2,1,0:T(8,128)(2,1)} %g2.1, ...), custom_call_target="tpu_custom_call" | custom-call | flops 8000000000 | bytes 12582912 | tf_op jit(solution)/shard_map/front/pallas_call | solution.py:101
  21.0 91.7 %rest.1 = (bf16[16,64,256]{2,1,0:T(8,128)(2,1)}, f32[3,36,128]{2,1,0:T(8,128)}) custom-call(bf16[16,2,200,256]{3,2,1,0:T(8,128)(2,1)} %get-tuple-element.10.slots, s32[16,8,128]{2,1,0:T(8,128)} %get-tuple-element.11.meta, bf16[16,2,16,128]{3,2,1,0:T(8,128)(2,1)} %get-tuple-element.12.wts, bf16[12,14,14,256]{3,2,1,0:T(8,128)(2,1)} %g2.1, ...), custom_call_target="tpu_custom_call" | custom-call | tf_op jit(solution)/shard_map/rest/pallas_call | solution.py:529
  112.8 1.4 %slice_bitcast_fusion = (f32[4608]{0:T(1024)}, f32[4608]{0:T(1024)}, f32[4608]{0:T(1024)}) fusion(f32[3,36,128]{2,1,0:T(8,128)} %get-tuple-element.15), kind=kLoop, calls=%fused_computation | loop fusion | bytes 110592 | tf_op jit(solution)/shard_map/reshape;squeeze | solution.py:543
  114.2 1.9 %copy.18 = bf16[16,64,256]{2,1,0:T(8,128)(2,1)} copy(bf16[16,64,256]{2,1,0:T(8,128)(2,1)} %get-tuple-element.23) | data formatting | bytes 1048576

commit v4 on v3

v4 whole, which is shorter than its diff:
```python
import functools

import jax
import jax.numpy as jnp
from jax import lax
from jax.experimental import pallas as pl
from jax.experimental.pallas import tpu as pltpu
from jax.sharding import PartitionSpec as P

F32, BF = jnp.float32, jnp.bfloat16
MESH = pl.DeviceIdType.MESH
C = 256
NB, RB = 4, 240
SR = 200
M = NB * RB
TH, TW, PW = 16, 64, 80
FM = TH * PW
FROWS = 16 + 18 * PW + 16
GR = 144
NT = (((1,), (1,)), ((), ()))
VM = pltpu.CompilerParams(vmem_limit_bytes=60 << 20)


def whole(shape, space=pltpu.VMEM):
    return pl.BlockSpec(memory_space=space)


def fixed(shape):
    zeros = (0,) * len(shape)
    return pl.BlockSpec(shape, lambda *_: zeros, pipeline_mode=pl.Buffered(1))


def load_padded(dst, src, fn=None, first=0):
    for r in range(NB):
        for y in range(14):
            v = src[first + r, y]
            dst[pl.ds(16 + r * RB + y * 16, 14), :] = v if fn is None else fn(v)


def spread(x3, v):
    n = v.shape[0]
    x3[:, 256:512] = v[...]
    x3[pl.ds(1, n - 1), 0:256] = v[pl.ds(0, n - 1), :]
    x3[pl.ds(0, n - 1), 512:768] = v[pl.ds(1, n - 1), :]


def line_up(wt, w):
    for dy in range(3):
        for kk in range(3):
            wt[dy, :, kk * C : (kk + 1) * C] = w[dy, 2 - kk]


def conv_flipped(x3, wt, base, rows, pitch):
    acc = None
    for dy in range(3):
        t = lax.dot_general(x3[pl.ds(base + (1 - dy) * pitch, rows), :], wt[dy], NT, preferred_element_type=F32)
        acc = t if acc is None else acc + t
    return acc


def emit_groups(value, out, lead):
    for g in range(32):
        for j in range(value.shape[1] // 256):
            lo = value[g * 8 : (g + 1) * 8, j * 256 : j * 256 + 128]
            hi = value[g * 8 : (g + 1) * 8, j * 256 + 128 : (j + 1) * 256]
            both = jnp.concatenate([lo, hi], axis=0).astype(BF)
            out[lead, g // 8, g // 4 % 2, g % 4, j * 16 : (j + 1) * 16, :] = both


def position():
    return lax.axis_index("ty"), lax.axis_index("tx")


def announce(peers):
    barrier = pltpu.get_barrier_semaphore()
    for peer in peers:
        pl.semaphore_signal(barrier, inc=1, device_id=peer, device_id_type=MESH)


def remote(src, dst, send, recv, peer):
    return pltpu.make_async_remote_copy(src, dst, send, recv, device_id=peer, device_id_type=MESH)


def go(copies):
    for copy in copies:
        copy.start()
    return copies


def settle(copies):
    for copy in copies:
        copy.wait()


def summed(mine, got):
    return mine.astype(F32) + got[0].astype(F32) + got[1].astype(F32) + got[2].astype(F32)


AROUND = [(-1, -1), (-1, 0), (-1, 1), (0, -1), (0, 1), (1, -1), (1, 0), (1, 1)]
ROW = [(0, 1), (1, 0), (0, 3), (3, 0), (1, 1), (3, 3), (1, 3), (3, 1), (0, 2), (2, 0), (1, 2), (2, 1), (3, 2), (2, 3), (2, 2)]


def around(ty, tx):
    peer = {(a, b): (lax.rem(ty + a + 8, 8), lax.rem(tx + b + 16, 16)) for a, b in AROUND}
    there = {
        (a, b): (ty + a >= 0) & (ty + a < 8) & (tx + b >= 0) & (tx + b < 16) for a, b in AROUND
    }
    return peer, there


def axes(ty, tx):
    x, c, y, z = ty // 2, ty % 2, tx // 4, tx % 4
    other = (x * 2 + 1 - c, tx)
    px = [(lax.rem(x + k, 4) * 2 + c, tx) for k in (1, 2, 3)]
    py = [(ty, lax.rem(y + k, 4) * 4 + z) for k in (1, 2, 3)]
    pz = [(ty, y * 4 + lax.rem(z + k, 4)) for k in (1, 2, 3)]
    return x, c, y, z, other, px, py, pz


ROWS_FIRST = (False, False, True)
ARRIVALS = ((15, 16), (0, 4), (4, 8), (8, 12), (12, 14), (14, 15))
class Store:
    pass


def all_kernel(names, tgt, orow, ocol, rows, cols, pre, g2, feat, w2, w1, inp, grad, w, out, sums, *scratch):
    r = Store()
    for name, ref in zip(names, scratch):
        setattr(r, name, ref)
    ty, tx = position()
    peer, there = around(ty, tx)
    x, c, y, z, other, px, py, pz = axes(ty, tx)
    row = [(ty, lax.rem(y + dy, 4) * 4 + lax.rem(z + dz, 4)) for dy, dz in ROW]
    to = [q[1] for q in row]
    pairs = (
        (inp, r.inp), (pre, r.pre), (g2, r.g2), (w2, r.w2), (w1, r.w1), (feat, r.feat), (grad, r.grad), (w, r.w),
    )
    loads = go([pltpu.make_async_copy(src, dst, r.fetch.at[i]) for i, (src, dst) in enumerate(pairs)])
    near = [peer[p] for p in AROUND] + row + [other] + px
    announce(near)
    tile_in, col_out = r.inp, r.col_out
    loads[0].wait()
    col_out[...] = tile_in[:, TW - 1, :]
    hsend, hrecv = r.hsend, r.hrecv
    corner = tile_in.at[:, 0:16]
    given = (
        ((-1, -1), corner, r.n_belowright), ((-1, 0), tile_in, r.n_below), ((-1, 1), col_out, r.n_belowleft),
        ((0, -1), corner, r.n_right), ((0, 1), col_out, r.n_left),
        ((1, -1), tile_in.at[TH - 1, 0:16], r.n_upright), ((1, 0), tile_in.at[TH - 1], r.n_up), ((1, 1), col_out, r.n_upleft),
    )

    vb, vx, x3 = r.vb, r.vx, r.x3
    for buf in (vb, vx):
        buf[...] = jnp.zeros_like(buf)
    x3[0:16] = jnp.zeros((16, 3 * C), BF)
    x3[M + 16 :] = jnp.zeros((16, 3 * C), BF)
    rgc, wtl, slotbuf, wtsbuf, metabuf = r.rgc, r.wtl, r.slotbuf, r.wtsbuf, r.metabuf
    rgc[12] = jnp.zeros((SR, C), BF)
    wtl[...] = jnp.zeros_like(wtl)
    for n in range(12):
        wtl[n, :, 0:14] = rows[n]
        wtl[n, :, 16:30] = cols[n]
    settle(loads[1:5])
    line_up(r.wt2, r.w2)
    line_up(r.wt1, r.w1)

    def first(n, carry):
        load_padded(vb, r.g2, None, n * NB)
        load_padded(vx, r.pre, None, n * NB)
        spread(x3, vb)
        b2 = conv_flipped(x3, r.wt2, 16, M, 16)
        g1 = jnp.where(vx[pl.ds(16, M), :] > 0, b2, 0.0).astype(BF)
        r.g1[pl.ds(n * NB, NB)] = g1.reshape(NB, RB, C)
        vb[pl.ds(16, M), :] = g1
        spread(x3, vb)
        rg = conv_flipped(x3, r.wt1, 16, M, 16).astype(BF)
        for q in range(NB):
            for i in range(14):
                rgc[n * NB + q, pl.ds(i * 14, 14), :] = rg[q * RB + i * 16 : q * RB + i * 16 + 14]
        return carry

    first(0, 0)
    pl.semaphore_wait(pltpu.get_barrier_semaphore(), len(near))
    halo = go([remote(src, dst, hsend.at[i], hrecv.at[i], peer[p]) for i, (p, src, dst) in enumerate(given)])
    lax.fori_loop(1, 3, first, 0)
    lanes = lax.broadcasted_iota(jnp.int32, (8, 128), 1)
    targets = [tgt[n] for n in range(12)]
    ranks = []
    for n in range(12):
        rank = jnp.int32(0)
        for q in range(n):
            rank = rank + jnp.where(targets[q] == targets[n], 1, 0)
        ranks.append(targets[n] * 2 + rank)

    def pack(t, carry):
        letter = jnp.zeros((8, 128), jnp.int32)
        for k in range(2):
            n = jnp.int32(12)
            for q in range(12):
                n = jnp.where(ranks[q] == 2 * t + k, q, n)
            m = jnp.minimum(n, 11)
            slotbuf[t, k] = rgc[n]
            wtsbuf[t, k] = wtl[n]
            letter = jnp.where(lanes == 4 * k + 1, jnp.where(n < 12, orow[m], 0), letter)
            letter = jnp.where(lanes == 4 * k + 2, jnp.where(n < 12, ocol[m], 0), letter)
        metabuf[t] = letter
        return carry

    lax.fori_loop(0, 16, pack, 0)
    slots_in, meta_in, wts_in = r.slots_in, r.meta_in, r.wts_in
    letters = go([remote(metabuf.at[q], meta_in.at[i], r.msend.at[i], r.mrecv.at[i], row[i]) for i, q in enumerate(to)])
    letters += go([remote(wtsbuf.at[q], wts_in.at[i], r.wsend.at[i], r.wrecv.at[i], row[i]) for i, q in enumerate(to)])
    sent = go([remote(slotbuf.at[q], slots_in.at[i], r.asend.at[i], r.arecv.at[i], row[i]) for i, q in enumerate(to)])
    kept = go([
        pltpu.make_async_copy(slotbuf.at[tx], slots_in.at[15], r.keep.at[0]),
        pltpu.make_async_copy(metabuf.at[tx], meta_in.at[15], r.keep.at[1]),
        pltpu.make_async_copy(wtsbuf.at[tx], wts_in.at[15], r.keep.at[2]),
    ])

    acc2, acc1, hparts = r.acc2, r.acc1, r.hparts
    for buf in (acc2, acc1):
        buf[...] = jnp.zeros_like(buf)
    settle(loads[5:])

    def step(n, carry):
        load_padded(vx, r.pre, lambda v: jnp.maximum(v, 0), n * NB)
        spread(x3, vx)
        load_padded(vb, r.g2, None, n * NB)
        gt = vb[pl.ds(16, M), :].T
        for dy in range(3):
            acc2[:, dy * 768 : (dy + 1) * 768] += jnp.dot(gt, x3[pl.ds(dy * 16, M), :], preferred_element_type=F32)
        load_padded(vx, r.feat, None, n * NB)
        spread(x3, vx)
        gt = r.g1[pl.ds(n * NB, NB)].reshape(M, C).T
        for dy in range(3):
            acc1[:, dy * 768 : (dy + 1) * 768] += jnp.dot(gt, x3[pl.ds(dy * 16, M), :], preferred_element_type=F32)
        return carry

    lax.fori_loop(0, 3, step, 0)
    emit_groups(acc1, hparts, 0)
    emit_groups(acc2, hparts, 1)
    swap = go([remote(hparts.at[:, :, 1 - c], r.hr0, r.ssend.at[0], r.srecv.at[0], other)])

    settle(letters)
    settle(kept)
    listed = pltpu.make_async_copy(meta_in, r.smeta, r.listed)
    listed.start()
    smeta, canvas, wp, rl, cl = r.smeta, r.canvas, r.wp, r.rl, r.cl
    canvas[...] = jnp.zeros_like(canvas)
    r.by_z[...] = jnp.zeros_like(r.by_z)
    wp[...] = jnp.zeros_like(wp)
    lane = lax.broadcasted_iota(jnp.int32, (128, 256), 1)
    at = lax.broadcasted_iota(jnp.int32, (128, 256), 0)
    bin_row = lane // 14
    bin_col = lane - bin_row * 14
    used = lane < 196
    both_w = wts_in[...].reshape(512, 128)
    rl[...] = jnp.dot(both_w, (used & (bin_row == at)).astype(BF), preferred_element_type=F32).reshape(32, 16, 256)
    cl[...] = jnp.dot(both_w, (used & (bin_col + 16 == at)).astype(BF), preferred_element_type=F32).reshape(32, 16, 256)
    for h in range(2):
        canvas[h, 0:TH, 0:TW, :] = r.grad[:, :, h * 128 : (h + 1) * 128].astype(F32)
    settle(swap)
    ha1 = r.ha1
    for xx in range(4):
        ha1[:, xx] = (hparts[:, xx, c].astype(F32) + r.hr0[:, xx].astype(F32)).astype(BF)
    cross = go([remote(ha1.at[:, lax.rem(x + k, 4)], r.hr1.at[k - 1], r.ssend.at[k], r.srecv.at[k], px[k - 1]) for k in (1, 2, 3)])
    settle(halo)
    strip, x3e, x3f, wt, fg_pad = r.strip, r.x3e, r.x3f, r.wt, r.fg_pad

    def kept_if(p, value):
        return jnp.where(there[p], value.astype(F32), 0.0).astype(BF)

    left_in = [jnp.where(there[p], q[...].astype(F32), 0.0) for p, q in (
        ((-1, -1), r.n_upleft), ((0, -1), r.n_left), ((1, -1), r.n_belowleft))]
    strip[0:16] = jnp.zeros((16, C), BF)
    strip[16 : 16 + TW] = kept_if((-1, 0), r.n_up[...])
    strip[16 + TW : 16 + PW] = kept_if((-1, 1), r.n_upright[...])
    for v in range(TH):
        base = 16 + (v + 1) * PW
        strip[base : base + TW] = tile_in[v]
        strip[base + TW : base + PW] = kept_if((0, 1), r.n_right[v])
        base += TH * PW
        strip[base : base + TW] = kept_if((1, 0), r.n_below[v])
        strip[base + TW : base + PW] = kept_if((1, 1), r.n_belowright[v])
    strip[16 + 33 * PW :] = jnp.zeros((PW + 16, C), BF)
    spread(x3e, strip)
    first_row = lax.broadcasted_iota(jnp.int32, (16, C), 0) == 0
    for v in range(-1, 32):
        edge = left_in[0][15:16] if v < 0 else left_in[1][v : v + 1] if v < TH else left_in[2][v - TH : v - TH + 1]
        base = 16 + (v + 1) * PW
        x3e[base : base + 16, 0:C] = jnp.where(first_row, edge, x3e[base : base + 16, 0:C].astype(F32)).astype(BF)
    line_up(wt, r.w)
    fg_pad[FROWS - 16 :, :] = jnp.zeros((16, C), BF)
    listed.wait()

    def put(s, carry):
        i, k = s // 2, s % 2
        top = 15 - smeta[i, 0, 4 * k + 1]
        side = TW - smeta[i, 0, 4 * k + 2]
        both = (rl[s][:, None, :] * cl[s][None, :, :]).reshape(256, 256).astype(BF)
        win = jnp.dot(both[:, 0:196], slots_in[i, k, 0:196, :], preferred_element_type=F32)
        for h in range(2):
            wp[h, 15:31, TW : TW + 16, :] = win[:, h * 128 : (h + 1) * 128].reshape(16, 16, 128)
        for v in range(31):
            for h in range(2):
                canvas[h, v] += wp[h, top + v, pl.ds(side, PW), :]
        return carry

    for n, (first, last) in enumerate(ARRIVALS):
        if n:
            for i in range(first, last):
                sent[i].wait_recv()
        lax.fori_loop(2 * first, 2 * last, put, 0)
        if n == 1:
            settle(cross)
            half = r.half
            half[...] = summed(ha1[:, x], r.hr1).astype(BF)
            hy = go([remote(half.at[:, lax.rem(y + k, 4)], r.rh.at[k - 1], r.ysend.at[k - 1], r.yrecv.at[k - 1], py[k - 1]) for k in (1, 2, 3)])

    p_down, p_right, p_diag, kcol, row0 = r.p_down, r.p_right, r.p_diag, r.kcol, r.row0
    for h in range(2):
        part = slice(h * 128, (h + 1) * 128)
        p_down[:, :, part] = canvas[h, TH - 1 : 31, 0:TW, :].astype(BF)
        p_right[:, :, part] = canvas[h, 0 : TH + 1, TW:PW, :].astype(BF)
        p_diag[:, :, part] = canvas[h, TH - 1 : 31, TW:PW, :].astype(BF)
        for n, col in enumerate((0, TW - 1, TW)):
            kcol[n, :, part] = canvas[h, :, col, :].astype(BF)
        row0[:, part] = canvas[h, 0, 0:TW, :].astype(BF)
    tsend, trecv = r.tsend, r.trecv
    r_down = r.r_down
    r_right = r.r_right
    r_diag = r.r_diag
    r_k = r.r_k
    r_row0 = r.r_row0
    r_s0 = r.r_s0
    tile = [
        remote(p_down, r_down, tsend.at[8], trecv.at[8], peer[(1, 0)]),
        remote(p_right, r_right, tsend.at[9], trecv.at[9], peer[(0, 1)]),
        remote(p_diag, r_diag, tsend.at[10], trecv.at[10], peer[(1, 1)]),
        remote(row0, r_row0, tsend.at[11], trecv.at[11], peer[(-1, 0)]),
        remote(p_right.at[0], r_s0, tsend.at[12], trecv.at[12], peer[(-1, 1)]),
    ]
    for i, (a, b) in enumerate(AROUND):
        src = kcol.at[0 if b < 0 else 1 if b > 0 else 2]
        tile.append(remote(src, r_k.at[7 - i], tsend.at[i], trecv.at[7 - i], peer[(a, b)]))
    go(tile)
    parts = r.parts
    r0 = r.r0
    a1 = r.a1
    ra = r.ra
    a2 = r.a2
    rb = r.rb
    a3 = r.a3
    rz = r.rz
    rh = r.rh
    a3h = r.a3h
    rzh = r.rzh
    total = r.total
    csend = r.csend
    crecv = r.crecv
    dsend = r.dsend
    drecv = r.drecv
    esend = r.esend
    erecv = r.erecv
    zsend = r.zsend
    zrecv = r.zrecv
    line_at = lax.broadcasted_iota(jnp.int32, (32, PW, 128), 0)
    col_at = lax.broadcasted_iota(jnp.int32, (32, PW, 128), 1)
    inside = ((line_at < TH) | there[(1, 0)]) & ((col_at < TW) | there[(0, 1)])
    for h in range(2):
        part = jnp.where(inside, canvas[h], 0.0).astype(BF).reshape(32 * PW, 128)
        r.whole_t[h * 128 : (h + 1) * 128, :] = part.T
    whole_t = r.whole_t[...]

    def term(q):
        emit_groups(jnp.dot(whole_t, x3e[pl.ds(16 + q * PW, 32 * PW), :], preferred_element_type=F32), parts, q)
        return go([remote(parts.at[q, :, 1 - c], r0.at[q], csend.at[q], crecv.at[q], other)])

    def first_axis(q, swap):
        settle(swap)
        a1[q] = (parts[q, :, c].astype(F32) + r0[q].astype(F32)).astype(BF)
        copies = []
        for k in (1, 2, 3):
            if ROWS_FIRST[q]:
                src, to = a1.at[q, lax.rem(x + k, 4)], px[k - 1]
            else:
                src, to = a1.at[q, :, lax.rem(y + k, 4)], py[k - 1]
            copies.append(remote(src, ra.at[q, k - 1], dsend.at[q * 3 + k - 1], drecv.at[q * 3 + k - 1], to))
        return go(copies)

    def second_axis(q, copies):
        mine = a1[q, x] if ROWS_FIRST[q] else a1[q, :, y]
        settle(copies)
        a2[q] = summed(mine, ra[q]).astype(BF)
        copies = []
        for k in (1, 2, 3):
            n, to = (lax.rem(y + k, 4), py[k - 1]) if ROWS_FIRST[q] else (lax.rem(x + k, 4), px[k - 1])
            copies.append(remote(a2.at[q, n], rb.at[q, k - 1], esend.at[q * 3 + k - 1], erecv.at[q * 3 + k - 1], to))
        return go(copies)

    def third_axis(q, copies):
        mine = a2[q, y] if ROWS_FIRST[q] else a2[q, x]
        settle(copies)
        a3[q] = summed(mine, rb[q]).astype(BF)
        return go([remote(a3.at[q], rz.at[q, k - 1], zsend.at[q * 3 + k - 1], zrecv.at[q * 3 + k - 1], pz[k - 1]) for k in (1, 2, 3)])

    s0 = term(0)
    s1 = term(1)
    settle(hy)
    total[0:2] = summed(half[:, y], rh)
    for t in range(2):
        for to_z in range(4):
            for bit in range(2):
                r.by_z[to_z, t, bit * 24 : bit * 24 + 18, :] = total[t, pl.ds(2 * to_z + bit, 18, stride=8), :]
    a3h[...] = r.by_z[...].astype(BF)
    hz = go([remote(a3h.at[lax.rem(z + k, 4)], rzh.at[k - 1], r.ysend.at[2 + k], r.yrecv.at[2 + k], pz[k - 1]) for k in (1, 2, 3)])
    f0 = first_axis(0, s0)
    s2 = term(2)
    f1 = first_axis(1, s1)
    f2 = first_axis(2, s2)
    settle(tile)

    up, left, right, below = there[(-1, 0)], there[(0, -1)], there[(0, 1)], there[(1, 0)]
    upleft, belowleft = there[(-1, -1)], there[(1, -1)]
    ks = {p: jnp.where(there[p], r_k[i].astype(F32), 0.0) for i, p in enumerate(AROUND)}
    own_k = kcol[2].astype(F32)
    at = lax.broadcasted_iota(jnp.int32, (16, C), 0)

    def low(v):
        s = jnp.zeros((1, C), F32)
        if 0 <= v:
            s += ks[(0, -1)][v : v + 1]
        if v <= 14:
            s += ks[(-1, -1)][16 + v : 17 + v]
        if v == 16:
            s += ks[(1, -1)][0:1]
        return s if v < 16 else jnp.where(below, s, 0.0)

    def high(v):
        s = jnp.zeros((1, C), F32)
        if 0 <= v:
            s += own_k[v : v + 1] + ks[(0, 1)][v : v + 1]
        if v <= 14:
            s += ks[(-1, 0)][16 + v : 17 + v] + ks[(-1, 1)][16 + v : 17 + v]
        if v == 16:
            s += ks[(1, 0)][0:1] + ks[(1, 1)][0:1]
        s = jnp.where(right, s, 0.0)
        return s if v < 16 else jnp.where(below, s, 0.0)

    for v in range(-2, 17):
        gap = jnp.zeros((16, C), F32)
        if v >= -1:
            gap = jnp.where(at == 0, high(v), gap)
        if v <= 15:
            gap = jnp.where(at == 15, low(v + 1), gap)
        fg_pad[pl.ds(16 + (v + 1) * PW + TW, 16), :] = gap.astype(BF)
    for v in range(-1, 17):
        for h in range(2):
            part = slice(h * 128, (h + 1) * 128)
            line = canvas[h, v, 0:TW, :] if v >= 0 else jnp.zeros((TW, 128), F32)
            side = jnp.zeros((16, 128), F32)
            if v <= 14:
                line = line + jnp.where(up, r_down[v + 1, :, part].astype(F32), 0.0)
                side += jnp.where(upleft, r_diag[v + 1, :, part].astype(F32), 0.0)
            if v >= 0:
                side += jnp.where(left, r_right[v, :, part].astype(F32), 0.0)
            if v == 16:
                line = line + r_row0[:, part].astype(F32)
                side += jnp.where(belowleft, r_s0[:, part].astype(F32), 0.0)
            first, others = line[0:16] + side, line[16:]
            if v == 16:
                first, others = jnp.where(below, first, 0.0), jnp.where(below, others, 0.0)
            base = 16 + (v + 1) * PW
            fg_pad[pl.ds(base, 16), part] = first.astype(BF)
            fg_pad[pl.ds(base + 16, TW - 16), part] = others.astype(BF)

    def conv(n):
        rows = FM // 2
        res = conv_flipped(x3f, wt, 16 + PW + n * rows, rows, PW).astype(BF).reshape(TH // 2, PW, C)
        out[n * TH // 2 : (n + 1) * TH // 2] = res[:, 0:TW, :]

    e0 = second_axis(0, f0)
    spread(x3f, fg_pad)
    e1 = second_axis(1, f1)
    conv(0)
    e2 = second_axis(2, f2)
    z0 = third_axis(0, e0)
    z1 = third_axis(1, e1)
    conv(1)
    z2 = third_axis(2, e2)
    for copy in sent:
        copy.wait_send()
    settle(hz)
    heads = summed(a3h[z], rzh)
    for t in range(2):
        for bit in range(2):
            sums[t, bit * 18 : (bit + 1) * 18, :] = heads[t, bit * 24 : bit * 24 + 18, :]
    for q, copies in enumerate((z0, z1, z2)):
        settle(copies)
        total[2, q * 48 : (q + 1) * 48] = summed(a3[q], rz[q])
    for bit in range(2):
        sums[2, bit * 18 : (bit + 1) * 18, :] = total[2, pl.ds(2 * z + bit, 18, stride=8), :]


def run_all(tgt, orow, ocol, rows, cols, pre, g2, feat, w2, w1, inp, grad, w):
    hbm = whole(None, pltpu.HBM)
    vm = whole(None)
    dma = pltpu.SemaphoreType.DMA
    regions = (12, 14, 14, C)
    s = Store()
    s.inp = pltpu.VMEM((TH, TW, C), BF)
    s.pre = pltpu.VMEM(regions, BF)
    s.g2 = pltpu.VMEM(regions, BF)
    s.feat = pltpu.VMEM(regions, BF)
    s.g1 = pltpu.VMEM((12, RB, C), BF)
    s.grad = pltpu.VMEM((TH, TW, C), BF)
    s.w = pltpu.VMEM((3, 3, C, C), BF)
    s.w2 = pltpu.VMEM((3, 3, C, C), BF)
    s.w1 = pltpu.VMEM((3, 3, C, C), BF)
    s.wt2 = pltpu.VMEM((3, C, 3 * C), BF)
    s.wt1 = pltpu.VMEM((3, C, 3 * C), BF)
    s.rgc = pltpu.VMEM((13, SR, C), BF)
    s.wtl = pltpu.VMEM((13, 16, 128), BF)
    s.slotbuf = pltpu.VMEM((16, 2, SR, C), BF)
    s.wtsbuf = pltpu.VMEM((16, 2, 16, 128), BF)
    s.slots_in = pltpu.VMEM((16, 2, SR, C), BF)
    s.wts_in = pltpu.VMEM((16, 2, 16, 128), BF)
    s.vb = pltpu.VMEM((M + 32, C), BF)
    s.vx = pltpu.VMEM((M + 32, C), BF)
    s.x3 = pltpu.VMEM((M + 32, 3 * C), BF)
    s.hparts = pltpu.VMEM((2, 4, 2, 4, GR, 128), BF)
    s.hr0 = pltpu.VMEM((2, 4, 4, GR, 128), BF)
    s.ha1 = pltpu.VMEM((2, 4, 4, GR, 128), BF)
    s.hr1 = pltpu.VMEM((3, 2, 4, GR, 128), BF)
    s.half = pltpu.VMEM((2, 4, GR, 128), BF)
    s.rh = pltpu.VMEM((3, 2, GR, 128), BF)
    s.a3h = pltpu.VMEM((4, 2, 48, 128), BF)
    s.rzh = pltpu.VMEM((3, 2, 48, 128), BF)
    s.col_out = pltpu.VMEM((TH, C), BF)
    s.n_belowright = pltpu.VMEM((TH, 16, C), BF)
    s.n_below = pltpu.VMEM((TH, TW, C), BF)
    s.n_belowleft = pltpu.VMEM((TH, C), BF)
    s.n_right = pltpu.VMEM((TH, 16, C), BF)
    s.n_left = pltpu.VMEM((TH, C), BF)
    s.n_upright = pltpu.VMEM((16, C), BF)
    s.n_up = pltpu.VMEM((TW, C), BF)
    s.n_upleft = pltpu.VMEM((TH, C), BF)
    s.p_down = pltpu.VMEM((TH, TW, C), BF)
    s.p_right = pltpu.VMEM((TH + 1, 16, C), BF)
    s.p_diag = pltpu.VMEM((TH, 16, C), BF)
    s.kcol = pltpu.VMEM((3, 32, C), BF)
    s.row0 = pltpu.VMEM((TW, C), BF)
    s.r_down = pltpu.VMEM((TH, TW, C), BF)
    s.r_right = pltpu.VMEM((TH + 1, 16, C), BF)
    s.r_diag = pltpu.VMEM((TH, 16, C), BF)
    s.r_k = pltpu.VMEM((8, 32, C), BF)
    s.r_row0 = pltpu.VMEM((TW, C), BF)
    s.r_s0 = pltpu.VMEM((16, C), BF)
    s.strip = pltpu.VMEM((32 + 34 * PW, C), BF)
    s.x3e = pltpu.VMEM((32 + 34 * PW, 3 * C), BF)
    s.whole_t = pltpu.VMEM((C, 32 * PW), BF)
    s.fg_pad = pltpu.VMEM((FROWS, C), BF)
    s.x3f = pltpu.VMEM((FROWS, 3 * C), BF)
    s.wt = pltpu.VMEM((3, C, 3 * C), BF)
    s.parts = pltpu.VMEM((3, 4, 2, 4, 48, 128), BF)
    s.r0 = pltpu.VMEM((3, 4, 4, 48, 128), BF)
    s.a1 = pltpu.VMEM((3, 4, 4, 48, 128), BF)
    s.ra = pltpu.VMEM((3, 3, 4, 48, 128), BF)
    s.a2 = pltpu.VMEM((3, 4, 48, 128), BF)
    s.rb = pltpu.VMEM((3, 3, 48, 128), BF)
    s.a3 = pltpu.VMEM((3, 48, 128), BF)
    s.rz = pltpu.VMEM((3, 3, 48, 128), BF)
    s.acc2 = pltpu.VMEM((C, 9 * C), F32)
    s.acc1 = pltpu.VMEM((C, 9 * C), F32)
    s.canvas = pltpu.VMEM((2, 2 * TH, PW, 128), F32)
    s.wp = pltpu.VMEM((2, 46, 144, 128), F32)
    s.rl = pltpu.VMEM((32, 16, 256), F32)
    s.cl = pltpu.VMEM((32, 16, 256), F32)
    s.total = pltpu.VMEM((3, GR, 128), F32)
    s.by_z = pltpu.VMEM((4, 2, 48, 128), F32)
    s.metabuf = pltpu.VMEM((16, 8, 128), jnp.int32)
    s.meta_in = pltpu.VMEM((16, 8, 128), jnp.int32)
    s.smeta = pltpu.SMEM((16, 8, 128), jnp.int32)
    s.fetch = dma((8,))
    s.msend = dma((15,))
    s.mrecv = dma((15,))
    s.wsend = dma((15,))
    s.wrecv = dma((15,))
    s.asend = dma((15,))
    s.arecv = dma((15,))
    s.hsend = dma((8,))
    s.hrecv = dma((8,))
    s.keep = dma((3,))
    s.ssend = dma((4,))
    s.srecv = dma((4,))
    s.ysend = dma((6,))
    s.yrecv = dma((6,))
    s.tsend = dma((13,))
    s.trecv = dma((13,))
    s.csend = dma((3,))
    s.crecv = dma((3,))
    s.dsend = dma((9,))
    s.drecv = dma((9,))
    s.esend = dma((9,))
    s.erecv = dma((9,))
    s.zsend = dma((9,))
    s.zrecv = dma((9,))
    s.listed = dma(())
    return pl.pallas_call(
        functools.partial(all_kernel, list(vars(s))),
        in_specs=[whole(None, pltpu.SMEM)] * 3 + [vm] * 2 + [hbm] * 8,
        out_specs=[vm] * 2,
        out_shape=[jax.ShapeDtypeStruct((TH, TW, C), BF), jax.ShapeDtypeStruct((3, 36, 128), F32)],
        scratch_shapes=list(vars(s).values()),
        compiler_params=pltpu.CompilerParams(vmem_limit_bytes=63 << 20, collective_id=1, has_side_effects=True),
        name="run_all",
    )(tgt, orow, ocol, rows, cols, pre, g2, feat, w2, w1, inp, grad, w)


def local(roi_feat, pre_one, grad_two, w_one, w_two, roi_rows, roi_cols, target_col, off_row, off_col, fpn_input, fpn_grad, w_fpn):
    grad_in, sums = run_all(
        target_col[:, 0], off_row, off_col, roi_rows, roi_cols, pre_one, grad_two, roi_feat, w_two, w_one, fpn_input, fpn_grad, w_fpn
    )
    return grad_in, sums[0].reshape(-1), sums[1].reshape(-1), sums[2].reshape(-1)


def solution(mesh):
    both = ("ty", "tx")
    placed = (
        P(both, None, None, None),
        P(both, None, None, None),
        P(both, None, None, None),
        P(),
        P(),
        P(both, None, None),
        P(both, None, None),
        P(both, None),
        P(both),
        P(both),
        P("ty", "tx", None),
        P("ty", "tx", None),
        P(),
    )
    return jax.shard_map(
        local,
        mesh=mesh,
        in_specs=placed,
        out_specs=(P("ty", "tx", None), P(both), P(both), P(both)),
        check_vma=False,
    )
```

time: 116 us -> 97.4 us (0.84)
  Pallas kernels: 112 us -> 93.3 us
    pallas_call x2 -> x1, Pallas kernels: 112 us -> 93.3 us  [run_all(): pl.pallas_call(functools.partial(all_kernel, list(vars(s))), in_specs=[wh...]
where the time goes in v4:
time: 97.4 us; the launch traced here: 97.2 us
  Pallas kernels  93.3 us (96%)
  local copies, waits for them, and re-layouts  3.27 us (3%)
    pallas_call x1, Pallas kernels, run_all(): pl.pallas_call(functools.partial(all_kernel, list(vars(s))), in_specs=[wh...  93.3 us

profile of v4, /device:TPU:0, one launch (start us, length us, event | category | flops | bytes accessed | tf_op | source)
XLA Modules:
  0.0 97.2 jit_solution(13338770611741227998)
XLA Ops:
  0.6 93.3 %run_all.1 = (bf16[16,64,256]{2,1,0:T(8,128)(2,1)}, f32[3,36,128]{2,1,0:T(8,128)}) custom-call(s32[12]{0:T(128)} %bitcast.7, s32[12]{0:T(128)} %orow.1, s32[12]{0:T(128)} %ocol.1, bf16[12,16,14]{2,1,0:T(8,128)(2,1)} %rows.1, bf16[12,16,14]{2,1,0:T(8,128)(2,1)} %cols.1, bf16[12,14,14,256]{3,2,1,0:T(8,128)(2,1)} %pre.1, bf16[12,14,14,256]{3,2,1,0:T(8,128)(2,1)} %g2.1, ...), custom_call_target="tpu_custom_call" | custom-call | tf_op jit(solution)/shard_map/run_all/pallas_call | solution.py:609
  93.9 1.4 %slice_bitcast_fusion = (f32[4608]{0:T(1024)}, f32[4608]{0:T(1024)}, f32[4608]{0:T(1024)}) fusion(f32[3,36,128]{2,1,0:T(8,128)} %get-tuple-element.7), kind=kLoop, calls=%fused_computation | loop fusion | bytes 110592 | tf_op jit(solution)/shard_map/reshape;squeeze | solution.py:624
  95.3 1.9 %copy.18 = bf16[16,64,256]{2,1,0:T(8,128)(2,1)} copy(bf16[16,64,256]{2,1,0:T(8,128)(2,1)} %get-tuple-element.15) | data formatting | bytes 1048576

commit v5 on v4

--- a/solution.py
+++ b/solution.py
@@ -10,9 +10,10 @@
 F32, BF = jnp.float32, jnp.bfloat16
 MESH = pl.DeviceIdType.MESH
 C = 256
-NB, RB = 4, 240
-SR = 200
-M = NB * RB
+LINE = 12 * 16
+SPAN = 16 + 16 * LINE + 16
+CUT = 4
+SA, SB = 14 * CUT, 144
 TH, TW, PW = 16, 64, 80
 FM = TH * PW
 FROWS = 16 + 18 * PW + 16
@@ -30,11 +31,16 @@
     return pl.BlockSpec(shape, lambda *_: zeros, pipeline_mode=pl.Buffered(1))
 
 
-def load_padded(dst, src, fn=None, first=0):
-    for r in range(NB):
+def load_padded(dst, src):
+    for n in range(12):
         for y in range(14):
-            v = src[first + r, y]
-            dst[pl.ds(16 + r * RB + y * 16, 14), :] = v if fn is None else fn(v)
+            dst[pl.ds(16 + (y + 1) * LINE + n * 16, 14), :] = src[n, y]
+
+
+def spread_rows(x3, v, low, high, fn=None):
+    for kk in range(3):
+        rows = v[pl.ds(low + kk - 1, high - low), :]
+        x3[low:high, kk * C : (kk + 1) * C] = rows if fn is None else fn(rows)
 
 
 def spread(x3, v):
@@ -44,10 +50,12 @@
     x3[pl.ds(0, n - 1), 512:768] = v[pl.ds(1, n - 1), :]
 
 
-def line_up(wt, w):
-    for dy in range(3):
-        for kk in range(3):
-            wt[dy, :, kk * C : (kk + 1) * C] = w[dy, 2 - kk]
+def line_up(wt, w, sems):
+    return go([
+        pltpu.make_async_copy(w.at[dy, 2 - kk], wt.at[dy, :, kk * C : (kk + 1) * C], sems.at[3 * dy + kk])
+        for dy in range(3)
+        for kk in range(3)
+    ])
 
 
 def conv_flipped(x3, wt, base, rows, pitch):
@@ -58,13 +66,13 @@
     return acc
 
 
-def emit_groups(value, out, lead):
+def emit_groups(value, out, lead, base=0):
     for g in range(32):
         for j in range(value.shape[1] // 256):
             lo = value[g * 8 : (g + 1) * 8, j * 256 : j * 256 + 128]
             hi = value[g * 8 : (g + 1) * 8, j * 256 + 128 : (j + 1) * 256]
             both = jnp.concatenate([lo, hi], axis=0).astype(BF)
-            out[lead, g // 8, g // 4 % 2, g % 4, j * 16 : (j + 1) * 16, :] = both
+            out[lead, g // 8, g // 4 % 2, g % 4, base + j * 16 : base + (j + 1) * 16, :] = both
 
 
 def position():
@@ -118,7 +126,7 @@
 
 
 ROWS_FIRST = (False, False, True)
-ARRIVALS = ((15, 16), (0, 4), (4, 8), (8, 12), (12, 14), (14, 15))
+EARLY = 1
 class Store:
     pass
 
@@ -132,10 +140,12 @@
     x, c, y, z, other, px, py, pz = axes(ty, tx)
     row = [(ty, lax.rem(y + dy, 4) * 4 + lax.rem(z + dz, 4)) for dy, dz in ROW]
     to = [q[1] for q in row]
-    pairs = (
-        (inp, r.inp), (pre, r.pre), (g2, r.g2), (w2, r.w2), (w1, r.w1), (feat, r.feat), (grad, r.grad), (w, r.w),
-    )
-    loads = go([pltpu.make_async_copy(src, dst, r.fetch.at[i]) for i, (src, dst) in enumerate(pairs)])
+    pairs = ((inp, r.inp), (pre, r.pre), (g2, r.g2), (feat, r.feat), (grad, r.grad))
+    loads = go([pltpu.make_async_copy(src, dst, r.fetch.at[i]) for i, (src, dst) in enumerate(pairs[:3])])
+    taps2 = line_up(r.wt2, w2, r.fetch2)
+    taps1 = line_up(r.wt1, w1, r.fetch1)
+    loads += go([pltpu.make_async_copy(src, dst, r.fetch.at[3 + i]) for i, (src, dst) in enumerate(pairs[3:])])
+    taps = line_up(r.wt, w, r.fetch0)
     near = [peer[p] for p in AROUND] + row + [other] + px
     announce(near)
     tile_in, col_out = r.inp, r.col_out
@@ -149,96 +159,107 @@
         ((1, -1), tile_in.at[TH - 1, 0:16], r.n_upright), ((1, 0), tile_in.at[TH - 1], r.n_up), ((1, 1), col_out, r.n_upleft),
     )
 
-    vb, vx, x3 = r.vb, r.vx, r.x3
-    for buf in (vb, vx):
+    vb, vx, vg, x3, x3g = r.vb, r.vx, r.vg, r.x3, r.x3g
+    for buf in (vb, vx, vg):
         buf[...] = jnp.zeros_like(buf)
-    x3[0:16] = jnp.zeros((16, 3 * C), BF)
-    x3[M + 16 :] = jnp.zeros((16, 3 * C), BF)
-    rgc, wtl, slotbuf, wtsbuf, metabuf = r.rgc, r.wtl, r.slotbuf, r.wtsbuf, r.metabuf
-    rgc[12] = jnp.zeros((SR, C), BF)
+    rgcs, bufs, wtl, wtsbuf, metabuf = (r.rgc_a, r.rgc_b), (r.buf_a, r.buf_b), r.wtl, r.wtsbuf, r.metabuf
+    for rgc in rgcs:
+        rgc[12] = jnp.zeros(rgc.shape[1:], BF)
+    for n in range(12):
+        r.rgc_b[n, SB - 16 : SB, :] = jnp.zeros((16, C), BF)
     wtl[...] = jnp.zeros_like(wtl)
     for n in range(12):
         wtl[n, :, 0:14] = rows[n]
         wtl[n, :, 16:30] = cols[n]
-    settle(loads[1:5])
-    line_up(r.wt2, r.w2)
-    line_up(r.wt1, r.w1)
-
-    def first(n, carry):
-        load_padded(vb, r.g2, None, n * NB)
-        load_padded(vx, r.pre, None, n * NB)
-        spread(x3, vb)
-        b2 = conv_flipped(x3, r.wt2, 16, M, 16)
-        g1 = jnp.where(vx[pl.ds(16, M), :] > 0, b2, 0.0).astype(BF)
-        r.g1[pl.ds(n * NB, NB)] = g1.reshape(NB, RB, C)
-        vb[pl.ds(16, M), :] = g1
-        spread(x3, vb)
-        rg = conv_flipped(x3, r.wt1, 16, M, 16).astype(BF)
-        for q in range(NB):
-            for i in range(14):
-                rgc[n * NB + q, pl.ds(i * 14, 14), :] = rg[q * RB + i * 16 : q * RB + i * 16 + 14]
-        return carry
-
-    first(0, 0)
-    pl.semaphore_wait(pltpu.get_barrier_semaphore(), len(near))
-    halo = go([remote(src, dst, hsend.at[i], hrecv.at[i], peer[p]) for i, (p, src, dst) in enumerate(given)])
-    lax.fori_loop(1, 3, first, 0)
-    lanes = lax.broadcasted_iota(jnp.int32, (8, 128), 1)
+    settle(loads[1:3])
+    load_padded(vb, r.g2)
+    load_padded(vx, r.pre)
+    ends = (16, 16 + 16 * LINE)
+    spread_rows(x3, vb, *ends)
+
+    def back(first, count):
+        base = 16 + (first + 1) * LINE
+        b2 = conv_flipped(x3, r.wt2, base, count * LINE, LINE)
+        vg[pl.ds(base, count * LINE), :] = jnp.where(vx[pl.ds(base, count * LINE), :] > 0, b2, 0.0).astype(BF)
+
+    def down(first, count, rgc, start):
+        rg = conv_flipped(x3g, r.wt1, 16 + (first + 1) * LINE, count * LINE, LINE).astype(BF)
+        for n in range(12):
+            for i in range(count):
+                rgc[n, pl.ds((first + i - start) * 14, 14), :] = rg[i * LINE + n * 16 : i * LINE + n * 16 + 14]
+
     targets = [tgt[n] for n in range(12)]
-    ranks = []
+    places = []
     for n in range(12):
         rank = jnp.int32(0)
         for q in range(n):
             rank = rank + jnp.where(targets[q] == targets[n], 1, 0)
-        ranks.append(targets[n] * 2 + rank)
-
-    def pack(t, carry):
+        places.append(targets[n] * 2 + rank)
+
+    def region_of(t, k):
+        n = jnp.int32(12)
+        for q in range(12):
+            n = jnp.where(places[q] == 2 * t + k, q, n)
+        return n
+
+    def pack_a(t, carry):
         letter = jnp.zeros((8, 128), jnp.int32)
+        lanes = lax.broadcasted_iota(jnp.int32, (8, 128), 1)
         for k in range(2):
-            n = jnp.int32(12)
-            for q in range(12):
-                n = jnp.where(ranks[q] == 2 * t + k, q, n)
+            n = region_of(t, k)
             m = jnp.minimum(n, 11)
-            slotbuf[t, k] = rgc[n]
+            r.buf_a[t, k] = r.rgc_a[n]
             wtsbuf[t, k] = wtl[n]
             letter = jnp.where(lanes == 4 * k + 1, jnp.where(n < 12, orow[m], 0), letter)
             letter = jnp.where(lanes == 4 * k + 2, jnp.where(n < 12, ocol[m], 0), letter)
         metabuf[t] = letter
         return carry
 
-    lax.fori_loop(0, 16, pack, 0)
-    slots_in, meta_in, wts_in = r.slots_in, r.meta_in, r.wts_in
+    def pack_b(t, carry):
+        for k in range(2):
+            r.buf_b[t, k] = r.rgc_b[region_of(t, k)]
+        return carry
+
+    settle(taps2)
+    back(0, CUT + 1)
+    pl.semaphore_wait(pltpu.get_barrier_semaphore(), len(near))
+    halo = go([remote(src, dst, hsend.at[i], hrecv.at[i], peer[p]) for i, (p, src, dst) in enumerate(given)])
+    spread_rows(x3g, vg, 16, 16 + (CUT + 2) * LINE)
+    settle(taps1)
+    down(0, CUT, r.rgc_a, 0)
+    lax.fori_loop(0, 16, pack_a, 0)
+    meta_in, wts_in = r.meta_in, r.wts_in
     letters = go([remote(metabuf.at[q], meta_in.at[i], r.msend.at[i], r.mrecv.at[i], row[i]) for i, q in enumerate(to)])
     letters += go([remote(wtsbuf.at[q], wts_in.at[i], r.wsend.at[i], r.wrecv.at[i], row[i]) for i, q in enumerate(to)])
-    sent = go([remote(slotbuf.at[q], slots_in.at[i], r.asend.at[i], r.arecv.at[i], row[i]) for i, q in enumerate(to)])
+    sent = go([remote(r.buf_a.at[q], r.in_a.at[i], r.asend.at[i], r.arecv.at[i], row[i]) for i, q in enumerate(to)])
+    back(5, 5)
+    back(10, 4)
+    spread_rows(x3g, vg, 16 + (CUT + 2) * LINE, 16 + 16 * LINE)
+    down(4, 5, r.rgc_b, CUT)
+    down(9, 5, r.rgc_b, CUT)
+    lax.fori_loop(0, 16, pack_b, 0)
+    sent_b = go([remote(r.buf_b.at[q], r.in_b.at[i], r.bsend.at[i], r.brecv.at[i], row[i]) for i, q in enumerate(to)])
     kept = go([
-        pltpu.make_async_copy(slotbuf.at[tx], slots_in.at[15], r.keep.at[0]),
+        pltpu.make_async_copy(r.buf_a.at[tx], r.in_a.at[15], r.keep.at[0]),
+        pltpu.make_async_copy(r.buf_b.at[tx], r.in_b.at[15], r.keep.at[3]),
         pltpu.make_async_copy(metabuf.at[tx], meta_in.at[15], r.keep.at[1]),
         pltpu.make_async_copy(wtsbuf.at[tx], wts_in.at[15], r.keep.at[2]),
     ])
 
-    acc2, acc1, hparts = r.acc2, r.acc1, r.hparts
-    for buf in (acc2, acc1):
-        buf[...] = jnp.zeros_like(buf)
-    settle(loads[5:])
-
-    def step(n, carry):
-        load_padded(vx, r.pre, lambda v: jnp.maximum(v, 0), n * NB)
-        spread(x3, vx)
-        load_padded(vb, r.g2, None, n * NB)
-        gt = vb[pl.ds(16, M), :].T
+    hparts, gt = r.hparts, r.gt
+    settle(loads[3:])
+
+    def weights(lead, v):
+        gt[...] = v[pl.ds(16 + LINE, 14 * LINE), :].T
         for dy in range(3):
-            acc2[:, dy * 768 : (dy + 1) * 768] += jnp.dot(gt, x3[pl.ds(dy * 16, M), :], preferred_element_type=F32)
-        load_padded(vx, r.feat, None, n * NB)
-        spread(x3, vx)
-        gt = r.g1[pl.ds(n * NB, NB)].reshape(M, C).T
-        for dy in range(3):
-            acc1[:, dy * 768 : (dy + 1) * 768] += jnp.dot(gt, x3[pl.ds(dy * 16, M), :], preferred_element_type=F32)
-        return carry
-
-    lax.fori_loop(0, 3, step, 0)
-    emit_groups(acc1, hparts, 0)
-    emit_groups(acc2, hparts, 1)
+            part = jnp.dot(gt[...], x3[pl.ds(16 + dy * LINE, 14 * LINE), :], preferred_element_type=F32)
+            emit_groups(part, hparts, lead, dy * 48)
+
+    spread_rows(x3, vx, *ends, lambda v: jnp.maximum(v, 0))
+    weights(1, vb)
+    load_padded(vx, r.feat)
+    spread_rows(x3, vx, *ends)
+    weights(0, vg)
     swap = go([remote(hparts.at[:, :, 1 - c], r.hr0, r.ssend.at[0], r.srecv.at[0], other)])
 
     settle(letters)
@@ -251,9 +272,12 @@
     wp[...] = jnp.zeros_like(wp)
     lane = lax.broadcasted_iota(jnp.int32, (128, 256), 1)
     at = lax.broadcasted_iota(jnp.int32, (128, 256), 0)
-    bin_row = lane // 14
-    bin_col = lane - bin_row * 14
-    used = lane < 196
+    bin_at = jnp.where(lane < 64, lane, lane - 8)
+    bin_row = bin_at // 14
+    bin_col = bin_at - bin_row * 14
+    used = (lane < SA) | ((lane >= 64) & (lane < 204))
+    gbuf = r.gbuf
+    gbuf[...] = jnp.zeros_like(gbuf)
     both_w = wts_in[...].reshape(512, 128)
     rl[...] = jnp.dot(both_w, (used & (bin_row == at)).astype(BF), preferred_element_type=F32).reshape(32, 16, 256)
     cl[...] = jnp.dot(both_w, (used & (bin_col + 16 == at)).astype(BF), preferred_element_type=F32).reshape(32, 16, 256)
@@ -265,7 +289,7 @@
         ha1[:, xx] = (hparts[:, xx, c].astype(F32) + r.hr0[:, xx].astype(F32)).astype(BF)
     cross = go([remote(ha1.at[:, lax.rem(x + k, 4)], r.hr1.at[k - 1], r.ssend.at[k], r.srecv.at[k], px[k - 1]) for k in (1, 2, 3)])
     settle(halo)
-    strip, x3e, x3f, wt, fg_pad = r.strip, r.x3e, r.x3f, r.wt, r.fg_pad
+    strip, x3e, x3f, wt, fg_pad = vx, x3g, r.x3f, r.wt, r.fg_pad
 
     def kept_if(p, value):
         return jnp.where(there[p], value.astype(F32), 0.0).astype(BF)
@@ -282,14 +306,14 @@
         base += TH * PW
         strip[base : base + TW] = kept_if((1, 0), r.n_below[v])
         strip[base + TW : base + PW] = kept_if((1, 1), r.n_belowright[v])
-    strip[16 + 33 * PW :] = jnp.zeros((PW + 16, C), BF)
-    spread(x3e, strip)
+    strip[16 + 33 * PW : 32 + 34 * PW] = jnp.zeros((PW + 16, C), BF)
+    spread_rows(x3e, strip, 16, 16 + 34 * PW)
     first_row = lax.broadcasted_iota(jnp.int32, (16, C), 0) == 0
     for v in range(-1, 32):
         edge = left_in[0][15:16] if v < 0 else left_in[1][v : v + 1] if v < TH else left_in[2][v - TH : v - TH + 1]
         base = 16 + (v + 1) * PW
         x3e[base : base + 16, 0:C] = jnp.where(first_row, edge, x3e[base : base + 16, 0:C].astype(F32)).astype(BF)
-    line_up(wt, r.w)
+    settle(taps)
     fg_pad[FROWS - 16 :, :] = jnp.zeros((16, C), BF)
     listed.wait()
 
@@ -298,7 +322,9 @@
         top = 15 - smeta[i, 0, 4 * k + 1]
         side = TW - smeta[i, 0, 4 * k + 2]
         both = (rl[s][:, None, :] * cl[s][None, :, :]).reshape(256, 256).astype(BF)
-        win = jnp.dot(both[:, 0:196], slots_in[i, k, 0:196, :], preferred_element_type=F32)
+        gbuf[0:SA, :] = r.in_a[i, k]
+        gbuf[64 : 64 + SB, :] = r.in_b[i, k]
+        win = jnp.dot(both, gbuf[...], preferred_element_type=F32)
         for h in range(2):
             wp[h, 15:31, TW : TW + 16, :] = win[:, h * 128 : (h + 1) * 128].reshape(16, 16, 128)
         for v in range(31):
@@ -306,16 +332,20 @@
                 canvas[h, v] += wp[h, top + v, pl.ds(side, PW), :]
         return carry
 
-    for n, (first, last) in enumerate(ARRIVALS):
-        if n:
-            for i in range(first, last):
-                sent[i].wait_recv()
-        lax.fori_loop(2 * first, 2 * last, put, 0)
-        if n == 1:
-            settle(cross)
-            half = r.half
-            half[...] = summed(ha1[:, x], r.hr1).astype(BF)
-            hy = go([remote(half.at[:, lax.rem(y + k, 4)], r.rh.at[k - 1], r.ysend.at[k - 1], r.yrecv.at[k - 1], py[k - 1]) for k in (1, 2, 3)])
+    def pair(i, carry):
+        remote(r.buf_a.at[0], r.in_a.at[i], r.asend.at[i], r.arecv.at[i], row[0]).wait_recv()
+        remote(r.buf_b.at[0], r.in_b.at[i], r.bsend.at[i], r.brecv.at[i], row[0]).wait_recv()
+        put(2 * i, 0)
+        put(2 * i + 1, 0)
+        return carry
+
+    lax.fori_loop(30, 32, put, 0)
+    lax.fori_loop(0, EARLY, pair, 0)
+    settle(cross)
+    half = r.half
+    half[...] = summed(ha1[:, x], r.hr1).astype(BF)
+    hy = go([remote(half.at[:, lax.rem(y + k, 4)], r.rh.at[k - 1], r.ysend.at[k - 1], r.yrecv.at[k - 1], py[k - 1]) for k in (1, 2, 3)])
+    lax.fori_loop(EARLY, 15, pair, 0)
 
     p_down, p_right, p_diag, kcol, row0 = r.p_down, r.p_right, r.p_diag, r.kcol, r.row0
     for h in range(2):
@@ -488,7 +518,7 @@
     z1 = third_axis(1, e1)
     conv(1)
     z2 = third_axis(2, e2)
-    for copy in sent:
+    for copy in sent + sent_b:
         copy.wait_send()
     settle(hz)
     heads = summed(a3h[z], rzh)
@@ -512,22 +542,12 @@
     s.pre = pltpu.VMEM(regions, BF)
     s.g2 = pltpu.VMEM(regions, BF)
     s.feat = pltpu.VMEM(regions, BF)
-    s.g1 = pltpu.VMEM((12, RB, C), BF)
     s.grad = pltpu.VMEM((TH, TW, C), BF)
-    s.w = pltpu.VMEM((3, 3, C, C), BF)
-    s.w2 = pltpu.VMEM((3, 3, C, C), BF)
-    s.w1 = pltpu.VMEM((3, 3, C, C), BF)
     s.wt2 = pltpu.VMEM((3, C, 3 * C), BF)
     s.wt1 = pltpu.VMEM((3, C, 3 * C), BF)
-    s.rgc = pltpu.VMEM((13, SR, C), BF)
     s.wtl = pltpu.VMEM((13, 16, 128), BF)
-    s.slotbuf = pltpu.VMEM((16, 2, SR, C), BF)
     s.wtsbuf = pltpu.VMEM((16, 2, 16, 128), BF)
-    s.slots_in = pltpu.VMEM((16, 2, SR, C), BF)
     s.wts_in = pltpu.VMEM((16, 2, 16, 128), BF)
-    s.vb = pltpu.VMEM((M + 32, C), BF)
-    s.vx = pltpu.VMEM((M + 32, C), BF)
-    s.x3 = pltpu.VMEM((M + 32, 3 * C), BF)
     s.hparts = pltpu.VMEM((2, 4, 2, 4, GR, 128), BF)
     s.hr0 = pltpu.VMEM((2, 4, 4, GR, 128), BF)
     s.ha1 = pltpu.VMEM((2, 4, 4, GR, 128), BF)
@@ -556,8 +576,6 @@
     s.r_k = pltpu.VMEM((8, 32, C), BF)
     s.r_row0 = pltpu.VMEM((TW, C), BF)
     s.r_s0 = pltpu.VMEM((16, C), BF)
-    s.strip = pltpu.VMEM((32 + 34 * PW, C), BF)
-    s.x3e = pltpu.VMEM((32 + 34 * PW, 3 * C), BF)
     s.whole_t = pltpu.VMEM((C, 32 * PW), BF)
     s.fg_pad = pltpu.VMEM((FROWS, C), BF)
     s.x3f = pltpu.VMEM((FROWS, 3 * C), BF)
@@ -570,8 +588,6 @@
     s.rb = pltpu.VMEM((3, 3, 48, 128), BF)
     s.a3 = pltpu.VMEM((3, 48, 128), BF)
     s.rz = pltpu.VMEM((3, 3, 48, 128), BF)
-    s.acc2 = pltpu.VMEM((C, 9 * C), F32)
-    s.acc1 = pltpu.VMEM((C, 9 * C), F32)
     s.canvas = pltpu.VMEM((2, 2 * TH, PW, 128), F32)
     s.wp = pltpu.VMEM((2, 46, 144, 128), F32)
     s.rl = pltpu.VMEM((32, 16, 256), F32)
@@ -581,7 +597,7 @@
     s.metabuf = pltpu.VMEM((16, 8, 128), jnp.int32)
     s.meta_in = pltpu.VMEM((16, 8, 128), jnp.int32)
     s.smeta = pltpu.SMEM((16, 8, 128), jnp.int32)
-    s.fetch = dma((8,))
+    s.fetch = dma((5,))
     s.msend = dma((15,))
     s.mrecv = dma((15,))
     s.wsend = dma((15,))
@@ -590,7 +606,7 @@
     s.arecv = dma((15,))
     s.hsend = dma((8,))
     s.hrecv = dma((8,))
-    s.keep = dma((3,))
+    s.keep = dma((4,))
     s.ssend = dma((4,))
     s.srecv = dma((4,))
     s.ysend = dma((6,))
@@ -606,6 +622,24 @@
     s.zsend = dma((9,))
     s.zrecv = dma((9,))
     s.listed = dma(())
+    s.vb = pltpu.VMEM((SPAN, C), BF)
+    s.vx = pltpu.VMEM((SPAN, C), BF)
+    s.vg = pltpu.VMEM((SPAN, C), BF)
+    s.x3 = pltpu.VMEM((SPAN, 3 * C), BF)
+    s.x3g = pltpu.VMEM((SPAN, 3 * C), BF)
+    s.gt = pltpu.VMEM((C, 14 * LINE), BF)
+    s.rgc_a = pltpu.VMEM((13, SA, C), BF)
+    s.rgc_b = pltpu.VMEM((13, SB, C), BF)
+    s.buf_a = pltpu.VMEM((16, 2, SA, C), BF)
+    s.buf_b = pltpu.VMEM((16, 2, SB, C), BF)
+    s.in_a = pltpu.VMEM((16, 2, SA, C), BF)
+    s.in_b = pltpu.VMEM((16, 2, SB, C), BF)
+    s.gbuf = pltpu.VMEM((256, C), BF)
+    s.fetch0 = dma((9,))
+    s.fetch1 = dma((9,))
+    s.fetch2 = dma((9,))
+    s.bsend = dma((15,))
+    s.brecv = dma((15,))
     return pl.pallas_call(
         functools.partial(all_kernel, list(vars(s))),
         in_specs=[whole(None, pltpu.SMEM)] * 3 + [vm] * 2 + [hbm] * 8,

time: 97.4 us -> 93.7 us (0.962)
  Pallas kernels: 93.3 us -> 89.5 us
    pallas_call x1, Pallas kernels: 93.3 us -> 89.5 us  [run_all(): pl.pallas_call(functools.partial(all_kernel, list(vars(s))), in_specs=[wh...]
where the time goes in v5:
time: 93.7 us; the launch traced here: 93.4 us
  Pallas kernels  89.5 us (96%)
  local copies, waits for them, and re-layouts  3.27 us (3%)
    pallas_call x1, Pallas kernels, run_all(): pl.pallas_call(functools.partial(all_kernel, list(vars(s))), in_specs=[wh...  89.5 us
    unnamed x1, local copies, waits for them, and re-layouts  1.88 us

profile of v5, /device:TPU:0, one launch (start us, length us, event | category | flops | bytes accessed | tf_op | source)
XLA Modules:
  0.0 93.4 jit_solution(8032200097916202367)
XLA Ops:
  0.6 89.5 %run_all.1 = (bf16[16,64,256]{2,1,0:T(8,128)(2,1)}, f32[3,36,128]{2,1,0:T(8,128)}) custom-call(s32[12]{0:T(128)} %bitcast.7, s32[12]{0:T(128)} %orow.1, s32[12]{0:T(128)} %ocol.1, bf16[12,16,14]{2,1,0:T(8,128)(2,1)} %rows.1, bf16[12,16,14]{2,1,0:T(8,128)(2,1)} %cols.1, bf16[12,14,14,256]{3,2,1,0:T(8,128)(2,1)} %pre.1, bf16[12,14,14,256]{3,2,1,0:T(8,128)(2,1)} %g2.1, ...), custom_call_target="tpu_custom_call" | custom-call | tf_op jit(solution)/shard_map/run_all/pallas_call | solution.py:643
  90.2 1.4 %slice_bitcast_fusion = (f32[4608]{0:T(1024)}, f32[4608]{0:T(1024)}, f32[4608]{0:T(1024)}) fusion(f32[3,36,128]{2,1,0:T(8,128)} %get-tuple-element.7), kind=kLoop, calls=%fused_computation | loop fusion | bytes 110592 | tf_op jit(solution)/shard_map/reshape;squeeze | solution.py:658
  91.5 1.9 %copy.18 = bf16[16,64,256]{2,1,0:T(8,128)(2,1)} copy(bf16[16,64,256]{2,1,0:T(8,128)(2,1)} %get-tuple-element.15) | data formatting | bytes 1048576
